TPU v7x, 32 devices: a whole 2x2x4 slice. The times are simulated.
32 devices in a mesh: groups: 2 (over x), kv: 16 (over z, y, core).
Axes of the slice: x: 2, y: 2, z: 4, core: 2. Of those that a mesh axis runs over, the one named last changes fastest.
Arguments:
- query_in: bfloat16 [256, 2048], P(('groups', 'kv')), parts along dimension 0, may hold values from -6 to 6
- key_in: bfloat16 [256, 512], P(('groups', 'kv')), parts along dimension 0, may hold values from -16 to 16
- value_in: bfloat16 [256, 512], P(('groups', 'kv')), parts along dimension 0, may hold values from -6 to 6
- cache_keys: bfloat16 [4, 6144, 512], P('groups', 'kv'), parts along dimension 0, may hold values from -700 to 700
- cache_values: bfloat16 [4, 6144, 512], P('groups', 'kv'), parts along dimension 0, may hold values from -6 to 6
- live_slots: int32 [4, 16], P('groups', 'kv'), parts along dimension 0, may hold values from 0 to 384, as said below
- span_starts: int32 [4], P('groups'), parts along dimension 0, may hold values from 0 to 1048447
Outputs:
- attended: bfloat16 [256, 2048], P(('groups', 'kv')), parts along dimension 0
There are 2 independent parts, one for each index of `groups`. A program takes and returns all parts, laid end to end along the dimension named above; each array names one. Nothing has to cross between parts.
Inputs may be any that keep to these rules, and one draw needn't show every extreme that they name: `live_slots`: in every block some device has all 384 of its slots live.
All inputs are finite; a program needn't handle non-finite values.
Results may differ from a plain program's by a relative error of at most 0.006.
The roundings to bfloat16 on the way count: a program that leaves them out, or rounds other values in their place, can miss the bound.
Values may be sent and summed in bfloat16 or wider, within the bound.
No kernel may reach another device: no remote copies, remote signals or barrier semaphores. Data moves between devices by JAX's collectives and lax.ppermute only.
A program may use at most 320 MiB of HBM per device.

v0:
```python
import functools

import jax
import jax.numpy as jnp
import numpy as np
from jax import lax
from jax.experimental import pallas as pl
from jax.experimental.pallas import tpu as pltpu
from jax.sharding import PartitionSpec as P


HD = 128
LANES = 128
NEG_FILL = -1e30
MAX_FLOOR = -5e29
LOG2E = 1.4426950408889634
PREPARE_FLOPS = 10_000_000_000
BF = jnp.bfloat16
F32 = jnp.float32


def turn_table(head_size):
    half_size = head_size // 2
    frequency = 500000.0 ** (-np.arange(half_size) * 2.0 / head_size)
    turn_counts = np.floor(frequency / (2.0 * np.pi) * 2.0**32 + 0.5).astype(np.int64) % 2**32
    turn_counts = np.where(turn_counts >= 2**31, turn_counts - 2**32, turn_counts)
    return turn_counts.astype(np.int32)


def stages_of(devices):
    core = 2 if devices % 2 == 0 else 1
    rest = devices // core
    inner = 1 << ((rest.bit_length() - 1) // 2)
    outer = rest // inner
    return (core * inner, outer), (core, inner), (1, core)


def swap(values, distance):
    devices = lax.axis_size("kv")
    return lax.ppermute(values, "kv", [(i, i ^ distance) for i in range(devices)])


def rotate(values, cosine, signed_sine):
    return values * cosine + pltpu.roll(values, HD // 2, 1) * signed_sine


def split_pair(values):
    high = values.astype(BF).astype(F32)
    return high, (values - high).astype(BF).astype(F32)


def split_index(values, size):
    if size & (size - 1) == 0:
        return values >> (size.bit_length() - 1), values & (size - 1)
    quotient = lax.div(values, jnp.int32(size))
    return quotient, values - quotient * size


def prepare_kernel(share, span_len, stages, *refs):
    (live_ref, start_ref, turn_ref, query_in, key_in, query_out, key_out, cos_ref, sin_ref, offset_ref, limit_ref) = refs
    (outer_stride, outer), (inner_stride, inner), (core_stride, core) = stages
    spans = live_ref.shape[0]
    me = lax.axis_index("kv")
    own_span, _ = split_index(me * share, span_len)
    query_out[...] = query_in[...]
    for relative in range(spans):
        limit_ref[relative : relative + 1, :] = jnp.full((1, LANES), live_ref[own_span ^ relative], jnp.int32)
    row = lax.broadcasted_iota(jnp.int32, cos_ref.shape, 0)
    member, within = split_index(row, share)
    member, high = split_index(member, outer)
    side, low = split_index(member, inner)
    distance = high * outer_stride + low * inner_stride + side * core_stride
    token = (me ^ distance) * share + within
    span, step = split_index(token, span_len)
    start = jnp.full(cos_ref.shape, start_ref[0], jnp.int32)
    for index in range(1, spans):
        start = jnp.where(span == index, start_ref[index], start)
    phases = (start + step) * turn_ref[...]
    angles = phases.astype(F32) * (2.0 * np.pi / 2.0**32)
    lane = lax.broadcasted_iota(jnp.int32, cos_ref.shape, 1)
    cos_ref[...] = jnp.cos(angles)
    sine = jnp.sin(angles)
    sin_ref[...] = jnp.where(lane < HD // 2, -sine, sine)
    offset_ref[...] = token - me * share
    for g in range(key_in.shape[1] // HD):
        lanes = slice(g * HD, (g + 1) * HD)
        key_out[:, lanes] = rotate(key_in[:, lanes].astype(F32), cos_ref[0:share, :], sin_ref[0:share, :]).astype(BF)


def prepare(span_len, stages, live, starts, query_in, key_in):
    vmem = pl.BlockSpec(memory_space=pltpu.VMEM)
    smem = pl.BlockSpec(memory_space=pltpu.SMEM)
    share = query_in.shape[0]
    rows = share * stages[0][1] * stages[1][1] * stages[2][1]
    spans = live.shape[0]
    turns = turn_table(HD)
    turns = jnp.asarray(np.concatenate([turns, turns])[None, :])
    like = [jax.ShapeDtypeStruct(array.shape, array.dtype) for array in (query_in, key_in)]
    table = jax.ShapeDtypeStruct((rows, HD), F32)
    return pl.pallas_call(
        functools.partial(prepare_kernel, share, span_len, stages),
        out_shape=(
            *like,
            table,
            table,
            jax.ShapeDtypeStruct((rows, HD), jnp.int32),
            jax.ShapeDtypeStruct((spans, LANES), jnp.int32),
        ),
        in_specs=[smem, smem, vmem, vmem, vmem],
        out_specs=(vmem,) * 6,
        cost_estimate=pl.CostEstimate(flops=PREPARE_FLOPS, bytes_accessed=12 * rows * HD, transcendentals=2 * rows * HD),
        compiler_params=pltpu.CompilerParams(vmem_limit_bytes=4 << 20),
        name="prepare",
    )(live, starts, turns, query_in, key_in)


def attend_kernel(blocks, heads, kv_heads, span_len, *refs):
    count = len(blocks)
    queries = refs[:count]
    (key_ref, cos_ref, sin_ref, offset_ref, limit_ref, value_ref, cache_k, cache_v) = refs[count : count + 8]
    outputs = refs[count + 8 :]
    share, slots = key_ref.shape[0], cache_k.shape[1]
    spans = cache_k.shape[0]
    group = heads // kv_heads
    scale = HD**-0.5 * LOG2E
    piece = queries[0].shape[0] // spans
    rows = piece * count
    own_span, _ = split_index(lax.axis_index("kv") * share, span_len)

    def pad(block):
        return jnp.concatenate([block.astype(F32), jnp.zeros((LANES - share, HD), F32)], axis=0).astype(BF)

    nt = (((1,), (1,)), ((), ()))
    parts = [slice(relative * piece, (relative + 1) * piece) for relative in range(spans)]
    tables = [
        [slice(block * queries[0].shape[0] + part.start, block * queries[0].shape[0] + part.stop) for block in blocks]
        for part in parts
    ]
    cells = [(relative, g) for relative in range(spans) for g in range(kv_heads)]
    slot = lax.broadcasted_iota(jnp.int32, (1, slots), 1)
    limits = [jnp.concatenate([limit_ref[part : part + 1, :]] * (slots // LANES), axis=1) for part in range(spans)]
    biases = [jnp.where(slot < limit, 0.0, NEG_FILL) for limit in limits]
    offset = jnp.concatenate([offset_ref[table, :] for table in tables[0]], axis=0)
    column = lax.broadcasted_iota(jnp.int32, (rows, LANES), 1)
    own_bias = jnp.where(jnp.logical_and(column <= offset, column < share), 0.0, NEG_FILL)
    own_bias = jnp.concatenate([own_bias] * group, axis=0)
    lane = lax.broadcasted_iota(jnp.int32, (rows, LANES), 1)

    raw, raw_own = {}, {}
    for relative, g in cells:
        stacked = []
        for h in range(g * group, (g + 1) * group):
            lanes = slice(h * HD, (h + 1) * HD)
            for source, table in zip(queries, tables[relative]):
                stacked.append(rotate(source[parts[relative], lanes].astype(F32), cos_ref[table, :], sin_ref[table, :]))
        query = jnp.concatenate(stacked, axis=0).astype(BF)
        lanes = slice(g * HD, (g + 1) * HD)
        raw[relative, g] = lax.dot_general(query, cache_k[own_span ^ relative, :, lanes], nt, preferred_element_type=F32)
        if relative == 0:
            raw_own[g] = lax.dot_general(query, pad(key_ref[:, lanes]), nt, preferred_element_type=F32)

    weights, own_weights, columns = {}, {}, {}
    for relative, g in cells:
        scores = raw[relative, g] * scale + biases[relative]
        top = jnp.max(scores, axis=1, keepdims=True)
        if relative == 0:
            own_scores = raw_own[g] * scale + own_bias
            top = jnp.maximum(top, jnp.max(own_scores, axis=1, keepdims=True))
        top_high, top_low = split_pair(jnp.maximum(top, MAX_FLOOR))
        top = top_high + top_low
        found = jnp.exp2(scores - top)
        total = jnp.sum(found, axis=1, keepdims=True)
        weights[relative, g] = found.astype(BF)
        if relative == 0:
            found = jnp.exp2(own_scores - top)
            total = total + jnp.sum(found, axis=1, keepdims=True)
            own_weights[g] = found.astype(BF)
        columns[relative, g] = (top_high, top_low, *split_pair(total))

    for relative, g in cells:
        lanes = slice(g * HD, (g + 1) * HD)
        summed = jnp.dot(weights[relative, g], cache_v[own_span ^ relative, :, lanes], preferred_element_type=F32)
        if relative == 0:
            summed = summed + jnp.dot(own_weights[g], pad(value_ref[:, lanes]), preferred_element_type=F32)
        for index in range(group):
            h = g * group + index
            for n, out in enumerate(outputs):
                at = index * rows + n * piece
                out[parts[relative], h * HD : (h + 1) * HD] = summed[at : at + piece].astype(BF)

    for relative in range(spans):
        stats = jnp.zeros((rows, LANES), F32)
        for g in range(kv_heads):
            for index in range(group):
                own = slice(index * rows, (index + 1) * rows)
                for place, values in enumerate(columns[relative, g]):
                    stats = jnp.where(lane == place * heads + g * group + index, values[own], stats)
        for n, out in enumerate(outputs):
            out[parts[relative], heads * HD :] = stats[n * piece : (n + 1) * piece].astype(BF)


def attend(blocks, heads, kv_heads, span_len, queries, held):
    vmem = pl.BlockSpec(memory_space=pltpu.VMEM)
    cache_k = held[-1]
    rows, slots = queries[0].shape[0], cache_k.shape[1]
    shape = jax.ShapeDtypeStruct((rows, heads * HD + LANES), BF)
    return pl.pallas_call(
        functools.partial(attend_kernel, blocks, heads, kv_heads, span_len),
        out_shape=(shape,) * len(queries),
        in_specs=[vmem] * (len(queries) + len(held)),
        out_specs=(vmem,) * len(queries),
        cost_estimate=pl.CostEstimate(
            flops=4 * len(queries) * rows * heads * HD * slots,
            bytes_accessed=4 * cache_k.size + 4 * len(queries) * rows * heads * HD,
            transcendentals=len(queries) * rows * heads * slots,
        ),
        compiler_params=pltpu.CompilerParams(vmem_limit_bytes=8 << 20),
        name="attend",
    )(*queries, *held)


def merge_kernel(groups, count, heads, last, *refs):
    outputs = refs[groups * count :]
    width = heads * HD
    sets = [refs[member * count : (member + 1) * count] for member in range(groups)]
    share = outputs[0].shape[0] // groups

    def store(member, lanes, values):
        for index, out in enumerate(outputs):
            out[member * share : (member + 1) * share, lanes] = values[index * share : (index + 1) * share].astype(BF)

    scaled = []
    for member, parts in enumerate(sets):
        pairs = []
        for part in parts:
            stats = part[:, width:].astype(F32)
            pairs.append(stats + pltpu.roll(stats, LANES - heads, 1))
        top = functools.reduce(jnp.maximum, pairs)
        factors = [jnp.exp2(own - top) for own in pairs]
        total = functools.reduce(
            jnp.add, [f * pltpu.roll(pair, LANES - 2 * heads, 1) for f, pair in zip(factors, pairs)]
        )
        if last:
            inverse = 1.0 / total
            factors = [f * inverse for f in factors]
        else:
            lane = lax.broadcasted_iota(jnp.int32, top.shape, 1)
            packed = jnp.zeros_like(top)
            for place, values in enumerate((*split_pair(top), *split_pair(total))):
                moved = pltpu.roll(values, place * heads, 1) if place else values
                packed = jnp.where(lane // heads == place, moved, packed)
            store(member, slice(width, width + LANES), packed)
        scaled.append(factors)
    for h in range(heads):
        lanes = slice(h * HD, (h + 1) * HD)
        for member, parts in enumerate(sets):
            terms = [f[:, h : h + 1] * part[:, lanes].astype(F32) for f, part in zip(scaled[member], parts)]
            store(member, lanes, functools.reduce(jnp.add, terms))


def merge(groups, pieces, heads, last=False):
    rows = groups[0][0].shape[0]
    count = len(groups[0])
    width = heads * HD + (0 if last else LANES)
    shape = jax.ShapeDtypeStruct((len(groups) * rows // pieces, width), BF)
    vmem = pl.BlockSpec(memory_space=pltpu.VMEM)
    total = len(groups) * count
    return pl.pallas_call(
        functools.partial(merge_kernel, len(groups), count, heads, last),
        out_shape=(shape,) * pieces,
        in_specs=[vmem] * total,
        out_specs=(vmem,) * pieces,
        cost_estimate=pl.CostEstimate(
            flops=4 * total * rows * heads * HD,
            bytes_accessed=2 * (total + len(groups)) * rows * width,
            transcendentals=total * rows * LANES,
        ),
        compiler_params=pltpu.CompilerParams(vmem_limit_bytes=4 << 20),
        name="merge",
    )(*[part for group in groups for part in group])


def per_device(query_in, key_in, value_in, cache_keys, cache_values, live_slots, span_starts):
    devices = lax.axis_size("kv")
    share = query_in.shape[0]
    span_count = span_starts.shape[0]
    span_len = share * devices // span_count
    heads = query_in.shape[1] // HD
    kv_heads = key_in.shape[1] // HD
    stages = stages_of(devices)
    (outer_stride, outer), (inner_stride, inner), (core_stride, core) = stages

    arrived = {k: swap(query_in, k * outer_stride) for k in range(1, outer)}
    query_own, *held = prepare(span_len, stages, live_slots.reshape(span_count), span_starts, query_in, key_in)
    held = [*held, value_in, cache_keys, cache_values]
    rows = jnp.concatenate([query_own] + [arrived[k] for k in range(1, outer)], axis=0)
    chunks = [rows] + [swap(rows, i * inner_stride) for i in range(1, inner)]
    groups = []
    for i, chunk in enumerate(chunks):
        other = swap(chunk, core_stride)
        if i == 0:
            even, odd = attend((i, inner + i), heads, kv_heads, span_len, (chunk, other), held)
        else:
            (even,) = attend((i,), heads, kv_heads, span_len, (chunk,), held)
            (odd,) = attend((inner + i,), heads, kv_heads, span_len, (other,), held)
        groups.append((even, swap(odd, core_stride)))
    kept = merge(groups, outer, heads)
    received = [swap(kept[k], k * outer_stride) for k in range(1, outer)]
    kept = merge([[kept[0]] + received], inner, heads)
    received = [swap(kept[k], k * inner_stride) for k in range(1, inner)]
    (attended,) = merge([[kept[0]] + received], 1, heads, last=True)
    return attended


def solution(mesh):
    in_specs = (
        P(("groups", "kv"), None),
        P(("groups", "kv"), None),
        P(("groups", "kv"), None),
        P("groups", "kv", None),
        P("groups", "kv", None),
        P("groups", "kv"),
        P("groups"),
    )
    out_specs = P(("groups", "kv"), None)
    return jax.shard_map(per_device, mesh=mesh, in_specs=in_specs, out_specs=out_specs, check_vma=False)
```

profile of v0, /device:TPU:0, one launch (start us, length us, event | category | flops | bytes accessed | tf_op | source)
XLA Modules:
  0.0 35.3 jit_solution(12453426422679872680)
XLA Ops:
  0.0 0.0 copy-start.7
  0.0 0.0 copy-start.5
  0.0 0.0 copy-start.6
  0.0 3.1 %collective-permute-start = (bf16[8,2048]{1,0:T(8,128)(2,1)}, bf16[8,2048]{1,0:T(8,128)(2,1)S(1)}, u32[]{:S(2)}, u32[]{:S(2)}) collective-permute-start(bf16[8,2048]{1,0:T(8,128)(2,1)} %refs_3_.1), channel_id=1, source_target_pairs={{0,4},{1,5},{2,6},{3,7},{4,0},{5,1},{6,2},{7,3},{8,12},{9,13},{10,... | collective-permute-start | bytes 98312 | tf_op jit(solution)/shard_map/ppermute | solution.py:40
  3.1 2.6 %collective-permute-start.1 = (bf16[8,2048]{1,0:T(8,128)(2,1)}, bf16[8,2048]{1,0:T(8,128)(2,1)S(1)}, u32[]{:S(2)}, u32[]{:S(2)}) collective-permute-start(bf16[8,2048]{1,0:T(8,128)(2,1)} %refs_3_.1), channel_id=1, source_target_pairs={{0,8},{1,9},{2,10},{3,11},{4,12},{5,13},{6,14},{7,15},{8,0},{9,1},... | collective-permute-start | bytes 98312 | tf_op jit(solution)/shard_map/ppermute | solution.py:40
  5.7 0.0 collective-permute-start.2
  5.7 0.0 copy-done.7
  5.7 0.0 copy-done.5
  5.7 0.0 copy-done.6
  5.7 0.0 copy-start.3
  5.7 0.8 %copy-done.3 = bf16[8,2048]{1,0:T(8,128)(2,1)S(1)} copy-done((bf16[8,2048]{1,0:T(8,128)(2,1)S(1)}, bf16[8,2048]{1,0:T(8,128)(2,1)}, u32[]{:S(2)}) %copy-start.3) | copy-done | bytes 32792
  6.5 0.0 copy-start.4
  6.5 0.7 %copy-done.4 = bf16[8,512]{1,0:T(8,128)(2,1)S(1)} copy-done((bf16[8,512]{1,0:T(8,128)(2,1)S(1)}, bf16[8,512]{1,0:T(8,128)(2,1)}, u32[]{:S(2)}) %copy-start.4) | copy-done | bytes 8216
  7.2 0.0 copy-start
  7.2 0.0 copy-start.1
  7.2 0.8 %prepare.1 = (bf16[8,2048]{1,0:T(8,128)(2,1)S(1)}, bf16[8,512]{1,0:T(8,128)(2,1)S(1)}, f32[128,128]{1,0:T(8,128)S(1)}, f32[128,128]{1,0:T(8,128)S(1)}, s32[128,128]{1,0:T(8,128)S(1)}, /*index=5*/s32[2,128]{1,0:T(2,128)S(1)}) custom-call(s32[2]{0:T(128)S(1)} %bitcast.1, s32[2]{0:T(128)S(1)} %copy-done.6, s32[1,128]{1,0:T(1,128)S(1)} %copy-done.7, ...), custom_call_target="tpu_custom_call" | custom-call | flops 10000000000 | bytes 196608 | tf_op jit(solution)/shard_map/prepare/pallas_call | solution.py:100
  8.1 0.0 collective-permute-done
  8.1 0.6 %collective-permute-done.1 = bf16[8,2048]{1,0:T(8,128)(2,1)S(1)} collective-permute-done((bf16[8,2048]{1,0:T(8,128)(2,1)}, bf16[8,2048]{1,0:T(8,128)(2,1)S(1)}, u32[]{:S(2)}, u32[]{:S(2)}) %collective-permute-start.1) | collective-permute-done | bytes 32800 | tf_op jit(solution)/shard_map/ppermute | solution.py:40
  8.7 2.9 %collective-permute-done.2 = bf16[8,2048]{1,0:T(8,128)(2,1)S(1)} collective-permute-done((bf16[8,2048]{1,0:T(8,128)(2,1)}, bf16[8,2048]{1,0:T(8,128)(2,1)S(1)}, u32[]{:S(2)}, u32[]{:S(2)}) %collective-permute-start.2) | collective-permute-done | bytes 32800 | tf_op jit(solution)/shard_map/ppermute | solution.py:40
  11.6 0.0 copy-start.2
  11.6 1.5 %collective-permute-start.5 = (bf16[32,2048]{1,0:T(8,128)(2,1)S(1)}, bf16[32,2048]{1,0:T(8,128)(2,1)S(1)}, u32[]{:S(2)}, u32[]{:S(2)}) collective-permute-start(bf16[32,2048]{1,0:T(8,128)(2,1)S(1)} %constant_dynamic-update-slice_fusion.refs_0_), channel_id=1, source_target_pairs={{0,2},{1,3},{2,0},{3,1},{4,6},{5,7},{6,4},{7,5},{8,10},{9,11},{10,... | collective-permute-start | bytes 393224 | tf_op jit(solution)/shard_map/ppermute | solution.py:40
  13.2 0.0 collective-permute-start.3
  13.2 3.4 %collective-permute-done.5.refs_0_ = bf16[32,2048]{1,0:T(8,128)(2,1)S(1)} collective-permute-done((bf16[32,2048]{1,0:T(8,128)(2,1)S(1)}, bf16[32,2048]{1,0:T(8,128)(2,1)S(1)}, u32[]{:S(2)}, u32[]{:S(2)}) %collective-permute-start.5) | collective-permute-done | bytes 131104 | tf_op jit(solution)/shard_map/ppermute | solution.py:40
  16.6 0.0 collective-permute-start.6
  16.6 0.0 collective-permute-done.3.refs_1_
  16.6 0.0 copy-done
  16.6 0.0 copy-done.1
  16.6 0.0 copy-done.2
  16.6 1.1 %attend.3 = (bf16[32,2176]{1,0:T(8,128)(2,1)S(1)}, bf16[32,2176]{1,0:T(8,128)(2,1)S(1)}) custom-call(bf16[32,2048]{1,0:T(8,128)(2,1)S(1)} %constant_dynamic-update-slice_fusion.refs_0_, bf16[32,2048]{1,0:T(8,128)(2,1)S(1)} %collective-permute-done.3.refs_1_, bf16[8,512]{1,0:T(8,128)(2,1)S(1)} %get-tuple-element.20.refs_2_.refs_1_, ...), custom_call_target="tpu_custom_call" | custom-call | flops 201326592 | bytes 2097152 | tf_op jit(solution)/shard_map/attend/pallas_call | solution.py:207
  17.8 0.6 %collective-permute-start.4 = (bf16[32,2176]{1,0:T(8,128)(2,1)S(1)}, bf16[32,2176]{1,0:T(8,128)(2,1)S(1)}, u32[]{:S(2)}, u32[]{:S(2)}) collective-permute-start(bf16[32,2176]{1,0:T(8,128)(2,1)S(1)} %get-tuple-element.26), channel_id=1, source_target_pairs={{0,1},{1,0},{2,3},{3,2},{4,5},{5,4},{6,7},{7,6},{8,9},{9,8},{10,11... | collective-permute-start | bytes 417800 | tf_op jit(solution)/shard_map/ppermute | solution.py:40
  18.4 0.0 collective-permute-done.6.refs_0_
  18.4 0.8 %attend.5 = bf16[32,2176]{1,0:T(8,128)(2,1)S(1)} custom-call(bf16[32,2048]{1,0:T(8,128)(2,1)S(1)} %collective-permute-done.6.refs_0_, bf16[8,512]{1,0:T(8,128)(2,1)S(1)} %get-tuple-element.20.refs_2_.refs_1_, f32[128,128]{1,0:T(8,128)S(1)} %get-tuple-element.21.refs_3_.refs_2_, f32[128,128]{1,0:T(8,128)S(1)} %get-tuple-element.22.refs_4_.refs_3_, ...), custom_call_target="tpu_custom_call" | custom-call | flops 100663296 | bytes 1835008 | tf_op jit(solution)/shard_map/attend/pallas_call | solution.py:207
  19.2 0.1 collective-permute-start.7
  19.3 0.8 %attend.4.refs_2_ = bf16[32,2176]{1,0:T(8,128)(2,1)S(1)} custom-call(bf16[32,2048]{1,0:T(8,128)(2,1)S(1)} %collective-permute-done.5.refs_0_, bf16[8,512]{1,0:T(8,128)(2,1)S(1)} %get-tuple-element.20.refs_2_.refs_1_, f32[128,128]{1,0:T(8,128)S(1)} %get-tuple-element.21.refs_3_.refs_2_, f32[128,128]{1,0:T(8,128)S(1)} %get-tuple-element.22.refs_4_.refs_3_, ...), custom_call_target="tpu_custom_call" | custom-call | flops 100663296 | bytes 1835008 | tf_op jit(solution)/shard_map/attend/pallas_call | solution.py:207
  20.1 0.0 collective-permute-done.4.refs_1_
  20.1 0.5 %collective-permute-done.7.refs_3_ = bf16[32,2176]{1,0:T(8,128)(2,1)S(1)} collective-permute-done((bf16[32,2176]{1,0:T(8,128)(2,1)S(1)}, bf16[32,2176]{1,0:T(8,128)(2,1)S(1)}, u32[]{:S(2)}, u32[]{:S(2)}) %collective-permute-start.7) | collective-permute-done | bytes 139296 | tf_op jit(solution)/shard_map/ppermute | solution.py:40
  20.6 0.5 %merge.3 = (bf16[16,2176]{1,0:T(8,128)(2,1)S(1)}, bf16[16,2176]{1,0:T(8,128)(2,1)S(1)}, bf16[16,2176]{1,0:T(8,128)(2,1)S(1)}, bf16[16,2176]{1,0:T(8,128)(2,1)S(1)}) custom-call(bf16[32,2176]{1,0:T(8,128)(2,1)S(1)} %get-tuple-element.25.refs_0_, bf16[32,2176]{1,0:T(8,128)(2,1)S(1)} %collective-permute-done.4.refs_1_, bf16[32,2176]{1,0:T(8,128)(2,1)S(1)} %attend.4.refs_2_, ...), custom_call_target="tpu_custom_call" | custom-call | flops 1048576 | bytes 835584 | tf_op jit(solution)/shard_map/merge/pallas_call | solution.py:268
  21.1 0.1 collective-permute-start.8
  21.2 0.9 %collective-permute-start.9 = (bf16[16,2176]{1,0:T(8,128)(2,1)S(1)}, bf16[16,2176]{1,0:T(8,128)(2,1)S(1)}, u32[]{:S(2)}, u32[]{:S(2)}) collective-permute-start(bf16[16,2176]{1,0:T(8,128)(2,1)S(1)} %get-tuple-element.29), channel_id=1, source_target_pairs={{0,8},{1,9},{2,10},{3,11},{4,12},{5,13},{6,14},{7,15},{8,0},{9,1},... | collective-permute-start | bytes 208904 | tf_op jit(solution)/shard_map/ppermute | solution.py:40
  22.1 3.4 %collective-permute-start.10 = (bf16[16,2176]{1,0:T(8,128)(2,1)S(1)}, bf16[16,2176]{1,0:T(8,128)(2,1)S(1)}, u32[]{:S(2)}, u32[]{:S(2)}) collective-permute-start(bf16[16,2176]{1,0:T(8,128)(2,1)S(1)} %get-tuple-element.30), channel_id=1, source_target_pairs={{0,12},{1,13},{2,14},{3,15},{4,8},{5,9},{6,10},{7,11},{8,4},{9,5},... | collective-permute-start | bytes 208904 | tf_op jit(solution)/shard_map/ppermute | solution.py:40
  25.5 0.9 %collective-permute-done.8.refs_1_ = bf16[16,2176]{1,0:T(8,128)(2,1)S(1)} collective-permute-done((bf16[16,2176]{1,0:T(8,128)(2,1)S(1)}, bf16[16,2176]{1,0:T(8,128)(2,1)S(1)}, u32[]{:S(2)}, u32[]{:S(2)}) %collective-permute-start.8) | collective-permute-done | bytes 69664 | tf_op jit(solution)/shard_map/ppermute | solution.py:40
  26.4 3.7 %collective-permute-done.9.refs_2_ = bf16[16,2176]{1,0:T(8,128)(2,1)S(1)} collective-permute-done((bf16[16,2176]{1,0:T(8,128)(2,1)S(1)}, bf16[16,2176]{1,0:T(8,128)(2,1)S(1)}, u32[]{:S(2)}, u32[]{:S(2)}) %collective-permute-start.9) | collective-permute-done | bytes 69664 | tf_op jit(solution)/shard_map/ppermute | solution.py:40
  30.1 0.0 collective-permute-done.10.refs_3_
  30.1 0.3 merge.4
  30.4 1.6 %collective-permute-start.11 = (bf16[8,2176]{1,0:T(8,128)(2,1)S(1)}, bf16[8,2176]{1,0:T(8,128)(2,1)S(1)}, u32[]{:S(2)}, u32[]{:S(2)}) collective-permute-start(bf16[8,2176]{1,0:T(8,128)(2,1)S(1)} %get-tuple-element.32), channel_id=1, source_target_pairs={{0,2},{1,3},{2,0},{3,1},{4,6},{5,7},{6,4},{7,5},{8,10},{9,11},{10,... | collective-permute-start | bytes 104456 | tf_op jit(solution)/shard_map/ppermute | solution.py:40
  32.0 2.4 %collective-permute-done.11.refs_1_ = bf16[8,2176]{1,0:T(8,128)(2,1)S(1)} collective-permute-done((bf16[8,2176]{1,0:T(8,128)(2,1)S(1)}, bf16[8,2176]{1,0:T(8,128)(2,1)S(1)}, u32[]{:S(2)}, u32[]{:S(2)}) %collective-permute-start.11) | collective-permute-done | bytes 34848 | tf_op jit(solution)/shard_map/ppermute | solution.py:40
  34.4 0.9 %merge.5 = bf16[8,2048]{1,0:T(8,128)(2,1)} custom-call(bf16[8,2176]{1,0:T(8,128)(2,1)S(1)} %get-tuple-element.31.refs_0_, bf16[8,2176]{1,0:T(8,128)(2,1)S(1)} %collective-permute-done.11.refs_1_), custom_call_target="tpu_custom_call" | custom-call | flops 131072 | bytes 98304 | tf_op jit(solution)/shard_map/merge/pallas_call | solution.py:268
  (4 shorter events, 0.0 us)
Async XLA Ops:
  0.0 5.7 %copy-start.7 = (s32[1,128]{1,0:T(1,128)S(1)}, s32[1,128]{1,0:T(1,128)}, u32[]{:S(2)}) copy-start(s32[1,128]{1,0:T(1,128)} %constant.2.clone.refs_2_) | copy-start | bytes 1540
  0.0 5.7 %copy-start.5 = (s32[2,1]{0,1:T(1,128)S(1)}, s32[2,1]{0,1:T(1,128)}, u32[]{:S(2)}) copy-start(s32[2,1]{0,1:T(1,128)} %param.13) | copy-start | bytes 28
  0.0 5.7 %copy-start.6 = (s32[2]{0:T(128)S(1)}, s32[2]{0:T(128)}, u32[]{:S(2)}) copy-start(s32[2]{0:T(128)} %refs_1_.1) | copy-start | bytes 28
  0.0 8.1 %collective-permute-start = (bf16[8,2048]{1,0:T(8,128)(2,1)}, bf16[8,2048]{1,0:T(8,128)(2,1)S(1)}, u32[]{:S(2)}, u32[]{:S(2)}) collective-permute-start(bf16[8,2048]{1,0:T(8,128)(2,1)} %refs_3_.1), channel_id=1, source_target_pairs={{0,4},{1,5},{2,6},{3,7},{4,0},{5,1},{6,2},{7,3},{8,12},{9,13},{10,... | collective-permute-start | bytes 98312 | tf_op jit(solution)/shard_map/ppermute | solution.py:40
  3.1 5.6 %collective-permute-start.1 = (bf16[8,2048]{1,0:T(8,128)(2,1)}, bf16[8,2048]{1,0:T(8,128)(2,1)S(1)}, u32[]{:S(2)}, u32[]{:S(2)}) collective-permute-start(bf16[8,2048]{1,0:T(8,128)(2,1)} %refs_3_.1), channel_id=1, source_target_pairs={{0,8},{1,9},{2,10},{3,11},{4,12},{5,13},{6,14},{7,15},{8,0},{9,1},... | collective-permute-start | bytes 98312 | tf_op jit(solution)/shard_map/ppermute | solution.py:40
  5.7 5.9 %collective-permute-start.2 = (bf16[8,2048]{1,0:T(8,128)(2,1)}, bf16[8,2048]{1,0:T(8,128)(2,1)S(1)}, u32[]{:S(2)}, u32[]{:S(2)}) collective-permute-start(bf16[8,2048]{1,0:T(8,128)(2,1)} %refs_3_.1), channel_id=1, source_target_pairs={{0,12},{1,13},{2,14},{3,15},{4,8},{5,9},{6,10},{7,11},{8,4},{9,5},... | collective-permute-start | bytes 98312 | tf_op jit(solution)/shard_map/ppermute | solution.py:40
  5.7 0.8 %copy-start.3 = (bf16[8,2048]{1,0:T(8,128)(2,1)S(1)}, bf16[8,2048]{1,0:T(8,128)(2,1)}, u32[]{:S(2)}) copy-start(bf16[8,2048]{1,0:T(8,128)(2,1)} %refs_3_.1) | copy-start | bytes 98308
  6.5 0.7 %copy-start.4 = (bf16[8,512]{1,0:T(8,128)(2,1)S(1)}, bf16[8,512]{1,0:T(8,128)(2,1)}, u32[]{:S(2)}) copy-start(bf16[8,512]{1,0:T(8,128)(2,1)} %refs_4_.1) | copy-start | bytes 24580
  7.2 9.4 %copy-start = (bf16[2,384,512]{2,1,0:T(8,128)(2,1)S(1)}, bf16[2,384,512]{2,1,0:T(8,128)(2,1)}, u32[]{:S(2)}) copy-start(bf16[2,384,512]{2,1,0:T(8,128)(2,1)} %refs_7_.5) | copy-start | bytes 2359300
  7.2 9.4 %copy-start.1 = (bf16[2,384,512]{2,1,0:T(8,128)(2,1)S(1)}, bf16[2,384,512]{2,1,0:T(8,128)(2,1)}, u32[]{:S(2)}) copy-start(bf16[2,384,512]{2,1,0:T(8,128)(2,1)} %refs_8_.5) | copy-start | bytes 2359300
  11.6 5.0 %copy-start.2 = (bf16[8,512]{1,0:T(8,128)(2,1)S(1)}, bf16[8,512]{1,0:T(8,128)(2,1)}, u32[]{:S(2)}) copy-start(bf16[8,512]{1,0:T(8,128)(2,1)} %refs_6_.3) | copy-start | bytes 24580
  11.6 5.0 %collective-permute-start.5 = (bf16[32,2048]{1,0:T(8,128)(2,1)S(1)}, bf16[32,2048]{1,0:T(8,128)(2,1)S(1)}, u32[]{:S(2)}, u32[]{:S(2)}) collective-permute-start(bf16[32,2048]{1,0:T(8,128)(2,1)S(1)} %constant_dynamic-update-slice_fusion.refs_0_), channel_id=1, source_target_pairs={{0,2},{1,3},{2,0},{3,1},{4,6},{5,7},{6,4},{7,5},{8,10},{9,11},{10,... | collective-permute-start | bytes 393224 | tf_op jit(solution)/shard_map/ppermute | solution.py:40
  13.2 3.5 %collective-permute-start.3 = (bf16[32,2048]{1,0:T(8,128)(2,1)S(1)}, bf16[32,2048]{1,0:T(8,128)(2,1)S(1)}, u32[]{:S(2)}, u32[]{:S(2)}) collective-permute-start(bf16[32,2048]{1,0:T(8,128)(2,1)S(1)} %constant_dynamic-update-slice_fusion.refs_0_), channel_id=1, source_target_pairs={{0,1},{1,0},{2,3},{3,2},{4,5},{5,4},{6,7},{7,6},{8,9},{9,8},{10,11... | collective-permute-start | bytes 393224 | tf_op jit(solution)/shard_map/ppermute | solution.py:40
  16.6 1.7 %collective-permute-start.6 = (bf16[32,2048]{1,0:T(8,128)(2,1)S(1)}, bf16[32,2048]{1,0:T(8,128)(2,1)S(1)}, u32[]{:S(2)}, u32[]{:S(2)}) collective-permute-start(bf16[32,2048]{1,0:T(8,128)(2,1)S(1)} %collective-permute-done.5.refs_0_), channel_id=1, source_target_pairs={{0,1},{1,0},{2,3},{3,2},{4,5},{5,4},{6,7},{7,6},{8,9},{9,8},{10,11... | collective-permute-start | bytes 393224 | tf_op jit(solution)/shard_map/ppermute | solution.py:40
  17.8 2.3 %collective-permute-start.4 = (bf16[32,2176]{1,0:T(8,128)(2,1)S(1)}, bf16[32,2176]{1,0:T(8,128)(2,1)S(1)}, u32[]{:S(2)}, u32[]{:S(2)}) collective-permute-start(bf16[32,2176]{1,0:T(8,128)(2,1)S(1)} %get-tuple-element.26), channel_id=1, source_target_pairs={{0,1},{1,0},{2,3},{3,2},{4,5},{5,4},{6,7},{7,6},{8,9},{9,8},{10,11... | collective-permute-start | bytes 417800 | tf_op jit(solution)/shard_map/ppermute | solution.py:40
  19.2 1.4 %collective-permute-start.7 = (bf16[32,2176]{1,0:T(8,128)(2,1)S(1)}, bf16[32,2176]{1,0:T(8,128)(2,1)S(1)}, u32[]{:S(2)}, u32[]{:S(2)}) collective-permute-start(bf16[32,2176]{1,0:T(8,128)(2,1)S(1)} %attend.5), channel_id=1, source_target_pairs={{0,1},{1,0},{2,3},{3,2},{4,5},{5,4},{6,7},{7,6},{8,9},{9,8},{10,11... | collective-permute-start | bytes 417800 | tf_op jit(solution)/shard_map/ppermute | solution.py:40
  21.1 5.3 %collective-permute-start.8 = (bf16[16,2176]{1,0:T(8,128)(2,1)S(1)}, bf16[16,2176]{1,0:T(8,128)(2,1)S(1)}, u32[]{:S(2)}, u32[]{:S(2)}) collective-permute-start(bf16[16,2176]{1,0:T(8,128)(2,1)S(1)} %get-tuple-element.28), channel_id=1, source_target_pairs={{0,4},{1,5},{2,6},{3,7},{4,0},{5,1},{6,2},{7,3},{8,12},{9,13},{10,... | collective-permute-start | bytes 208904 | tf_op jit(solution)/shard_map/ppermute | solution.py:40
  21.2 8.9 %collective-permute-start.9 = (bf16[16,2176]{1,0:T(8,128)(2,1)S(1)}, bf16[16,2176]{1,0:T(8,128)(2,1)S(1)}, u32[]{:S(2)}, u32[]{:S(2)}) collective-permute-start(bf16[16,2176]{1,0:T(8,128)(2,1)S(1)} %get-tuple-element.29), channel_id=1, source_target_pairs={{0,8},{1,9},{2,10},{3,11},{4,12},{5,13},{6,14},{7,15},{8,0},{9,1},... | collective-permute-start | bytes 208904 | tf_op jit(solution)/shard_map/ppermute | solution.py:40
  22.1 8.0 %collective-permute-start.10 = (bf16[16,2176]{1,0:T(8,128)(2,1)S(1)}, bf16[16,2176]{1,0:T(8,128)(2,1)S(1)}, u32[]{:S(2)}, u32[]{:S(2)}) collective-permute-start(bf16[16,2176]{1,0:T(8,128)(2,1)S(1)} %get-tuple-element.30), channel_id=1, source_target_pairs={{0,12},{1,13},{2,14},{3,15},{4,8},{5,9},{6,10},{7,11},{8,4},{9,5},... | collective-permute-start | bytes 208904 | tf_op jit(solution)/shard_map/ppermute | solution.py:40
  30.4 4.0 %collective-permute-start.11 = (bf16[8,2176]{1,0:T(8,128)(2,1)S(1)}, bf16[8,2176]{1,0:T(8,128)(2,1)S(1)}, u32[]{:S(2)}, u32[]{:S(2)}) collective-permute-start(bf16[8,2176]{1,0:T(8,128)(2,1)S(1)} %get-tuple-element.32), channel_id=1, source_target_pairs={{0,2},{1,3},{2,0},{3,1},{4,6},{5,7},{6,4},{7,5},{8,10},{9,11},{10,... | collective-permute-start | bytes 104456 | tf_op jit(solution)/shard_map/ppermute | solution.py:40
where the time goes:
time: 35.5 us; the launch traced here: 35.3 us
  waiting for transfers between devices  14.4 us (41%)
  starting transfers between devices  13.9 us (39%)
  Pallas kernels  5.28 us (15%)
  local copies, waits for them, and re-layouts  1.53 us (4%)
    ppermute x12, waiting for transfers between devices, swap(): lax.ppermute(values, 'kv', [(i, i ^ distance) for i in range(devices)])  14.4 us
    ppermute x12, starting transfers between devices, swap(): lax.ppermute(values, 'kv', [(i, i ^ distance) for i in range(devices)])  13.9 us
    pallas_call x3, Pallas kernels, attend(): pl.pallas_call(functools.partial(attend_kernel, blocks, heads, kv_heads,...  2.77 us
    pallas_call x3, Pallas kernels, merge(): pl.pallas_call(functools.partial(merge_kernel, len(groups), count, heads,...  1.67 us
    unnamed x19, local copies, waits for them, and re-layouts  1.53 us
    pallas_call x1, Pallas kernels, prepare(): pl.pallas_call(functools.partial(prepare_kernel, share, span_len, stages)...  0.84 us
  transfers between devices with their start and end apart: 12, of which 7 were waited for; matrix products, arithmetic and copies ran while one was open for 0% of the time, Pallas kernels for 10%

commit v1 on v0

v1 whole, which is shorter than its diff:
```python
import functools

import jax
import jax.numpy as jnp
import numpy as np
from jax import lax
from jax.experimental import pallas as pl
from jax.experimental.pallas import tpu as pltpu
from jax.sharding import PartitionSpec as P


HD = 128
LANES = 128
NEG_FILL = -1e30
MAX_FLOOR = -5e29
LOG2E = 1.4426950408889634
PREPARE_FLOPS = 10_000_000_000
BF = jnp.bfloat16
F32 = jnp.float32


def turn_table(head_size):
    half_size = head_size // 2
    frequency = 500000.0 ** (-np.arange(half_size) * 2.0 / head_size)
    turn_counts = np.floor(frequency / (2.0 * np.pi) * 2.0**32 + 0.5).astype(np.int64) % 2**32
    turn_counts = np.where(turn_counts >= 2**31, turn_counts - 2**32, turn_counts)
    return turn_counts.astype(np.int32)


def stages_of(devices):
    core = 2 if devices % 2 == 0 else 1
    rest = devices // core
    inner = 1 << ((rest.bit_length() - 1) // 2)
    outer = rest // inner
    return (core * inner, outer), (core, inner), (1, core)


def swap(values, distance):
    devices = lax.axis_size("kv")
    return lax.ppermute(values, "kv", [(i, i ^ distance) for i in range(devices)])


def rotate(values, cosine, signed_sine):
    return values * cosine + pltpu.roll(values, HD // 2, 1) * signed_sine


def split_pair(values):
    high = values.astype(BF).astype(F32)
    return high, (values - high).astype(BF).astype(F32)


def split_index(values, size):
    if size & (size - 1) == 0:
        return values >> (size.bit_length() - 1), values & (size - 1)
    quotient = lax.div(values, jnp.int32(size))
    return quotient, values - quotient * size


def prepare_kernel(share, span_len, stages, live_ref, start_ref, query_in, query_out, cos_ref, sin_ref, offset_ref, limit_ref):
    (outer_stride, outer), (inner_stride, inner), (core_stride, _) = stages
    spans = live_ref.shape[0]
    me = lax.axis_index("kv")
    own_span, _ = split_index(me * share, span_len)
    query_out[...] = query_in[...]
    for relative in range(spans):
        limit_ref[relative : relative + 1, :] = jnp.full((1, LANES), live_ref[own_span ^ relative], jnp.int32)
    lane = lax.broadcasted_iota(jnp.int32, (1, HD), 1)
    pair = jnp.where(lane < HD // 2, lane, lane - HD // 2)
    turns = jnp.zeros((1, HD), jnp.int32)
    for index, turn in enumerate(turn_table(HD)):
        turns = jnp.where(pair == index, jnp.int32(turn), turns)
    row = lax.broadcasted_iota(jnp.int32, cos_ref.shape, 0)
    member, within = split_index(row, share)
    low, high = split_index(member, outer)
    distance = jnp.where(low < inner, high * outer_stride + low * inner_stride, core_stride)
    token = (me ^ distance) * share + within
    span, step = split_index(token, span_len)
    start = jnp.full(cos_ref.shape, start_ref[0], jnp.int32)
    for index in range(1, spans):
        start = jnp.where(span == index, start_ref[index], start)
    angles = ((start + step) * turns).astype(F32) * (2.0 * np.pi / 2.0**32)
    cos_ref[...] = jnp.cos(angles)
    sine = jnp.sin(angles)
    sin_ref[...] = jnp.where(lane < HD // 2, -sine, sine)
    offset_ref[...] = token - me * share


def prepare(span_len, stages, live, starts, query_in):
    vmem = pl.BlockSpec(memory_space=pltpu.VMEM)
    smem = pl.BlockSpec(memory_space=pltpu.SMEM)
    share = query_in.shape[0]
    rows = share * (stages[0][1] * stages[1][1] + 1)
    spans = live.shape[0]
    table = jax.ShapeDtypeStruct((rows, HD), F32)
    whole = jax.ShapeDtypeStruct((rows, HD), jnp.int32)
    limits = jax.ShapeDtypeStruct((spans, LANES), jnp.int32)
    return pl.pallas_call(
        functools.partial(prepare_kernel, share, span_len, stages),
        out_shape=(jax.ShapeDtypeStruct(query_in.shape, BF), table, table, whole, limits),
        in_specs=[smem, smem, vmem],
        out_specs=(vmem,) * 5,
        cost_estimate=pl.CostEstimate(flops=PREPARE_FLOPS, bytes_accessed=12 * rows * HD, transcendentals=2 * rows * HD),
        compiler_params=pltpu.CompilerParams(vmem_limit_bytes=4 << 20),
        name="prepare",
    )(live, starts, query_in)


def attend_kernel(chunk, outer, core, core_stride, heads, kv_heads, span_len, earlier, *refs):
    query_ref, refs = refs[0], refs[1:]
    before, refs = refs[:earlier], refs[earlier:]
    (cos_ref, sin_ref, offset_ref), refs = refs[:3], refs[3:]
    sides = [refs[side * 5 : side * 5 + 5] for side in range(core)]
    outputs = refs[5 * core :]
    _, key_ref, _, cache_k, _ = sides[0]
    share, slots, spans = key_ref.shape[0], cache_k.shape[1], cache_k.shape[0]
    group = heads // kv_heads
    scale = HD**-0.5 * LOG2E
    total_rows = query_ref.shape[0]
    rows = total_rows // spans
    me = lax.axis_index("kv")
    own_span, _ = split_index(me * share, span_len)
    key_rows = [slice(0, share), slice(cos_ref.shape[0] - share, cos_ref.shape[0])]
    nt = (((1,), (1,)), ((), ()))
    cells = [(relative, g) for relative in range(spans) for g in range(kv_heads)]
    slot = lax.broadcasted_iota(jnp.int32, (1, slots), 1)
    biases = {}
    for relative in range(spans):
        for side in range(core):
            limit = jnp.concatenate([sides[side][0][relative : relative + 1, :]] * (slots // LANES), axis=1)
            biases[relative, side] = jnp.where(slot < limit, 0.0, NEG_FILL)
    lane = lax.broadcasted_iota(jnp.int32, (rows, LANES), 1)
    other = ((me ^ core_stride) - me) * share - share
    place = jnp.where(lane < share, lane, lane + other)
    offset = offset_ref[chunk * total_rows : chunk * total_rows + rows, :]
    admitted = jnp.logical_and(place <= offset, lane < core * share)
    own_bias = jnp.concatenate([jnp.where(admitted, 0.0, NEG_FILL)] * group, axis=0)

    def stack_new(blocks):
        filler = jnp.zeros((LANES - core * share, HD), F32)
        return jnp.concatenate([*blocks, filler], axis=0).astype(BF)

    raw, raw_own = {}, {}
    for relative, g in cells:
        span = own_span ^ relative
        part = slice(relative * rows, (relative + 1) * rows)
        table = slice(chunk * total_rows + relative * rows, chunk * total_rows + (relative + 1) * rows)
        cos, sin = cos_ref[table, :], sin_ref[table, :]
        stacked = []
        for h in range(g * group, (g + 1) * group):
            stacked.append(rotate(query_ref[part, h * HD : (h + 1) * HD].astype(F32), cos, sin))
        query = jnp.concatenate(stacked, axis=0).astype(BF)
        lanes = slice(g * HD, (g + 1) * HD)
        for side in range(core):
            raw[relative, g, side] = lax.dot_general(
                query, sides[side][3][span, :, lanes], nt, preferred_element_type=F32
            )
        if relative == 0:
            keys = stack_new(
                [
                    rotate(sides[side][1][:, lanes].astype(F32), cos_ref[key_rows[side], :], sin_ref[key_rows[side], :])
                    for side in range(core)
                ]
            )
            raw_own[g] = lax.dot_general(query, keys, nt, preferred_element_type=F32)

    weights, columns = {}, {}
    for relative, g in cells:
        scores = [raw[relative, g, side] * scale + biases[relative, side] for side in range(core)]
        if relative == 0:
            scores.append(raw_own[g] * scale + own_bias)
        top = functools.reduce(jnp.maximum, [jnp.max(values, axis=1, keepdims=True) for values in scores])
        top_high, top_low = split_pair(jnp.maximum(top, MAX_FLOOR))
        top = top_high + top_low
        found = [jnp.exp2(values - top) for values in scores]
        total = functools.reduce(jnp.add, [jnp.sum(values, axis=1, keepdims=True) for values in found])
        weights[relative, g] = [values.astype(BF) for values in found]
        columns[relative, g] = (top_high, top_low, *split_pair(total))

    def store(relative, lanes, values):
        if len(outputs) == 1:
            outputs[0][relative * rows : (relative + 1) * rows, lanes] = values.astype(BF)
        else:
            for index in range(outer // spans):
                outputs[relative * outer // spans + index][earlier * share : (earlier + 1) * share, lanes] = values[
                    index * share : (index + 1) * share
                ].astype(BF)

    for relative, g in cells:
        span = own_span ^ relative
        lanes = slice(g * HD, (g + 1) * HD)
        terms = [
            jnp.dot(weights[relative, g][side], sides[side][4][span, :, lanes], preferred_element_type=F32)
            for side in range(core)
        ]
        if relative == 0:
            values = stack_new([sides[side][2][:, lanes].astype(F32) for side in range(core)])
            terms.append(jnp.dot(weights[relative, g][core], values, preferred_element_type=F32))
        summed = functools.reduce(jnp.add, terms)
        for index in range(group):
            h = g * group + index
            store(relative, slice(h * HD, (h + 1) * HD), summed[index * rows : (index + 1) * rows])

    for relative in range(spans):
        stats = jnp.zeros((rows, LANES), F32)
        for g in range(kv_heads):
            for index in range(group):
                own = slice(index * rows, (index + 1) * rows)
                for place, values in enumerate(columns[relative, g]):
                    stats = jnp.where(lane == place * heads + g * group + index, values[own], stats)
        store(relative, slice(heads * HD, heads * HD + LANES), stats)
    for index, source in enumerate(before):
        for high, out in enumerate(outputs):
            out[index * share : (index + 1) * share, :] = (
                source[high * share : (high + 1) * share, :].astype(F32).astype(BF)
            )


def attend(chunk, stages, heads, kv_heads, span_len, query, before, tables, sides, last):
    vmem = pl.BlockSpec(memory_space=pltpu.VMEM)
    (_, outer), _, (core_stride, core) = stages
    rows, slots = query.shape[0], sides[0][3].shape[1]
    width = heads * HD + LANES
    if last:
        shape = (jax.ShapeDtypeStruct((rows // outer * (len(before) + 1), width), BF),) * outer
    else:
        shape = (jax.ShapeDtypeStruct((rows, width), BF),)
    operands = [query, *before, *tables, *[array for side in sides for array in side]]
    return pl.pallas_call(
        functools.partial(attend_kernel, chunk, outer, core, core_stride, heads, kv_heads, span_len, len(before)),
        out_shape=shape,
        in_specs=[vmem] * len(operands),
        out_specs=(vmem,) * len(shape),
        cost_estimate=pl.CostEstimate(
            flops=4 * core * rows * heads * HD * slots,
            bytes_accessed=4 * core * sides[0][3].size + 4 * rows * heads * HD,
            transcendentals=core * rows * heads * slots,
        ),
        compiler_params=pltpu.CompilerParams(vmem_limit_bytes=10 << 20),
        name="attend",
    )(*operands)


def merge_kernel(groups, count, heads, last, *refs):
    outputs = refs[groups * count :]
    width = heads * HD
    sets = [refs[member * count : (member + 1) * count] for member in range(groups)]
    share = outputs[0].shape[0] // groups

    def store(member, lanes, values):
        for index, out in enumerate(outputs):
            out[member * share : (member + 1) * share, lanes] = values[index * share : (index + 1) * share].astype(BF)

    scaled = []
    for member, parts in enumerate(sets):
        pairs = []
        for part in parts:
            stats = part[:, width:].astype(F32)
            pairs.append(stats + pltpu.roll(stats, LANES - heads, 1))
        top = functools.reduce(jnp.maximum, pairs)
        factors = [jnp.exp2(own - top) for own in pairs]
        total = functools.reduce(
            jnp.add, [f * pltpu.roll(pair, LANES - 2 * heads, 1) for f, pair in zip(factors, pairs)]
        )
        if last:
            inverse = 1.0 / total
            factors = [f * inverse for f in factors]
        else:
            lane = lax.broadcasted_iota(jnp.int32, top.shape, 1)
            packed = jnp.zeros_like(top)
            for place, values in enumerate((*split_pair(top), *split_pair(total))):
                moved = pltpu.roll(values, place * heads, 1) if place else values
                packed = jnp.where(lane // heads == place, moved, packed)
            store(member, slice(width, width + LANES), packed)
        scaled.append(factors)
    for h in range(heads):
        lanes = slice(h * HD, (h + 1) * HD)
        for member, parts in enumerate(sets):
            terms = [f[:, h : h + 1] * part[:, lanes].astype(F32) for f, part in zip(scaled[member], parts)]
            store(member, lanes, functools.reduce(jnp.add, terms))


def merge(groups, pieces, heads, last=False):
    rows = groups[0][0].shape[0]
    count = len(groups[0])
    width = heads * HD + (0 if last else LANES)
    shape = jax.ShapeDtypeStruct((len(groups) * rows // pieces, width), BF)
    vmem = pl.BlockSpec(memory_space=pltpu.VMEM)
    total = len(groups) * count
    return pl.pallas_call(
        functools.partial(merge_kernel, len(groups), count, heads, last),
        out_shape=(shape,) * pieces,
        in_specs=[vmem] * total,
        out_specs=(vmem,) * pieces,
        cost_estimate=pl.CostEstimate(
            flops=4 * total * rows * heads * HD,
            bytes_accessed=2 * (total + len(groups)) * rows * width,
            transcendentals=total * rows * LANES,
        ),
        compiler_params=pltpu.CompilerParams(vmem_limit_bytes=4 << 20),
        name="merge",
    )(*[part for group in groups for part in group])


def per_device(query_in, key_in, value_in, cache_keys, cache_values, live_slots, span_starts):
    devices = lax.axis_size("kv")
    share = query_in.shape[0]
    span_count = span_starts.shape[0]
    span_len = share * devices // span_count
    heads = query_in.shape[1] // HD
    kv_heads = key_in.shape[1] // HD
    stages = stages_of(devices)
    (outer_stride, outer), (inner_stride, inner), (core_stride, core) = stages

    arrived = {k: swap(query_in, k * outer_stride) for k in range(1, outer)}
    other_keys = swap(cache_keys, core_stride)
    other_values = swap(cache_values, core_stride)
    query_own, *tables, limits = prepare(span_len, stages, live_slots.reshape(span_count), span_starts, query_in)
    rows = jnp.concatenate([query_own] + [arrived[k] for k in range(1, outer)], axis=0)
    chunks = [rows] + [swap(rows, i * inner_stride) for i in range(1, inner)]
    sides = [(limits, key_in, value_in, cache_keys, cache_values)]
    small = [swap(array, core_stride) for array in (key_in, value_in, limits)]
    sides.append((small[2], small[0], small[1], other_keys, other_values))
    before = []
    for i, chunk in enumerate(chunks):
        last = i == inner - 1
        parts = attend(i, stages, heads, kv_heads, span_len, chunk, before if last else [], tables, sides, last)
        before += parts if not last else []
    received = [swap(parts[k], k * outer_stride) for k in range(1, outer)]
    kept = merge([[parts[0]] + received], inner, heads)
    received = [swap(kept[k], k * inner_stride) for k in range(1, inner)]
    (attended,) = merge([[kept[0]] + received], 1, heads, last=True)
    return attended


def solution(mesh):
    in_specs = (
        P(("groups", "kv"), None),
        P(("groups", "kv"), None),
        P(("groups", "kv"), None),
        P("groups", "kv", None),
        P("groups", "kv", None),
        P("groups", "kv"),
        P("groups"),
    )
    out_specs = P(("groups", "kv"), None)
    return jax.shard_map(per_device, mesh=mesh, in_specs=in_specs, out_specs=out_specs, check_vma=False)
```

time: 35.5 us -> 32.1 us (0.904)
  waiting for transfers between devices: 14.4 us -> 12.9 us
  local copies, waits for them, and re-layouts: 1.53 us -> 0.8 us
  Pallas kernels: 5.28 us -> 4.66 us
  starting transfers between devices: 13.9 us -> 13.4 us
    ppermute x12 -> x13, waiting for transfers between devices: 14.4 us -> 12.9 us  [swap(): lax.ppermute(values, 'kv', [(i, i ^ distance) for i in range(devices)])]
    unnamed x19 -> x17, local copies, waits for them, and re-layouts: 1.53 us -> 0.79 us
    ppermute x12 -> x13, starting transfers between devices: 13.9 us -> 13.4 us  [swap(): lax.ppermute(values, 'kv', [(i, i ^ distance) for i in range(devices)])]
    pallas_call x3 -> x2, Pallas kernels: 1.67 us -> 1.2 us  [merge(): pl.pallas_call(functools.partial(merge_kernel, len(groups), count, heads,...]
    pallas_call x3 -> x2, Pallas kernels: 2.77 us -> 2.72 us  [attend(): pl.pallas_call(functools.partial(attend_kernel, chunk, outer, core, core_...]
  transfers between devices with their start and end apart: 12 -> 13, of which waited for: 7 -> 6; matrix products, arithmetic and copies ran while one was open for 0% -> 0% of each run, Pallas kernels for 10% -> 7%
where the time goes in v1:
time: 32.1 us; the launch traced here: 31.9 us
  starting transfers between devices  13.4 us (42%)
  waiting for transfers between devices  12.9 us (40%)
  Pallas kernels  4.66 us (15%)
  local copies, waits for them, and re-layouts  0.8 us (2%)
    ppermute x13, starting transfers between devices, swap(): lax.ppermute(values, 'kv', [(i, i ^ distance) for i in range(devices)])  13.4 us
    ppermute x13, waiting for transfers between devices, swap(): lax.ppermute(values, 'kv', [(i, i ^ distance) for i in range(devices)])  12.9 us
    pallas_call x2, Pallas kernels, attend(): pl.pallas_call(functools.partial(attend_kernel, chunk, outer, core, core_...  2.72 us
    pallas_call x2, Pallas kernels, merge(): pl.pallas_call(functools.partial(merge_kernel, len(groups), count, heads,...  1.2 us
    unnamed x17, local copies, waits for them, and re-layouts  0.79 us
    pallas_call x1, Pallas kernels, prepare(): pl.pallas_call(functools.partial(prepare_kernel, share, span_len, stages)...  0.74 us
  transfers between devices with their start and end apart: 13, of which 6 were waited for; matrix products, arithmetic and copies ran while one was open for 0% of the time, Pallas kernels for 7%

profile of v1, /device:TPU:0, one launch (start us, length us, event | category | flops | bytes accessed | tf_op | source)
XLA Modules:
  0.0 31.9 jit_solution(17754950890232017648)
XLA Ops:
  0.0 0.0 copy-start.6
  0.0 0.0 copy-start.5
  0.0 3.1 %collective-permute-start = (bf16[8,2048]{1,0:T(8,128)(2,1)}, bf16[8,2048]{1,0:T(8,128)(2,1)S(1)}, u32[]{:S(2)}, u32[]{:S(2)}) collective-permute-start(bf16[8,2048]{1,0:T(8,128)(2,1)} %query_in.1), channel_id=1, source_target_pairs={{0,4},{1,5},{2,6},{3,7},{4,0},{5,1},{6,2},{7,3},{8,12},{9,13},{10,... | collective-permute-start | bytes 98312 | tf_op jit(solution)/shard_map/ppermute | solution.py:40
  3.1 2.5 %collective-permute-start.2 = (bf16[8,2048]{1,0:T(8,128)(2,1)}, bf16[8,2048]{1,0:T(8,128)(2,1)S(1)}, u32[]{:S(2)}, u32[]{:S(2)}) collective-permute-start(bf16[8,2048]{1,0:T(8,128)(2,1)} %query_in.1), channel_id=1, source_target_pairs={{0,12},{1,13},{2,14},{3,15},{4,8},{5,9},{6,10},{7,11},{8,4},{9,5},... | collective-permute-start | bytes 98312 | tf_op jit(solution)/shard_map/ppermute | solution.py:40
  5.5 0.1 collective-permute-start.1
  5.7 0.0 collective-permute-start.7
  5.7 0.5 %collective-permute-start.8 = (bf16[2,384,512]{2,1,0:T(8,128)(2,1)}, bf16[2,384,512]{2,1,0:T(8,128)(2,1)S(1)}, u32[]{:S(2)}, u32[]{:S(2)}) collective-permute-start(bf16[2,384,512]{2,1,0:T(8,128)(2,1)} %refs_9_.1), channel_id=1, source_target_pairs={{0,1},{1,0},{2,3},{3,2},{4,5},{5,4},{6,7},{7,6},{8,9},{9,8},{10,11... | collective-permute-start | bytes 2359304 | tf_op jit(solution)/shard_map/ppermute | solution.py:40
  6.2 0.0 copy-done.6
  6.2 0.0 copy-done.5
  6.2 0.0 copy-start.4
  6.2 0.8 %copy-done.4 = bf16[8,2048]{1,0:T(8,128)(2,1)S(1)} copy-done((bf16[8,2048]{1,0:T(8,128)(2,1)S(1)}, bf16[8,2048]{1,0:T(8,128)(2,1)}, u32[]{:S(2)}) %copy-start.4) | copy-done | bytes 32792
  6.9 0.0 copy-start
  6.9 0.0 copy-start.1
  6.9 0.7 %prepare.1 = (bf16[8,2048]{1,0:T(8,128)(2,1)S(1)}, f32[72,128]{1,0:T(8,128)S(1)}, f32[72,128]{1,0:T(8,128)S(1)}, s32[72,128]{1,0:T(8,128)S(1)}, s32[2,128]{1,0:T(2,128)S(1)}) custom-call(s32[2]{0:T(128)S(1)} %bitcast.1, s32[2]{0:T(128)S(1)} %copy-done.6, bf16[8,2048]{1,0:T(8,128)(2,1)S(1)} %copy-done.4), custom_call_target="tpu_custom_call" | custom-call | flops 10000000000 | bytes 110592 | tf_op jit(solution)/shard_map/prepare/pallas_call | solution.py:97
  7.7 0.0 collective-permute-done
  7.7 3.2 %collective-permute-done.1 = bf16[8,2048]{1,0:T(8,128)(2,1)S(1)} collective-permute-done((bf16[8,2048]{1,0:T(8,128)(2,1)}, bf16[8,2048]{1,0:T(8,128)(2,1)S(1)}, u32[]{:S(2)}, u32[]{:S(2)}) %collective-permute-start.1) | collective-permute-done | bytes 32800 | tf_op jit(solution)/shard_map/ppermute | solution.py:40
  10.9 0.0 copy-start.2
  10.9 0.0 copy-start.3
  10.9 0.0 collective-permute-done.2
  10.9 1.6 %collective-permute-start.3 = (bf16[32,2048]{1,0:T(8,128)(2,1)S(1)}, bf16[32,2048]{1,0:T(8,128)(2,1)S(1)}, u32[]{:S(2)}, u32[]{:S(2)}) collective-permute-start(bf16[32,2048]{1,0:T(8,128)(2,1)S(1)} %constant_dynamic-update-slice_fusion.refs_0_), channel_id=1, source_target_pairs={{0,2},{1,3},{2,0},{3,1},{4,6},{5,7},{6,4},{7,5},{8,10},{9,11},{10,... | collective-permute-start | bytes 393224 | tf_op jit(solution)/shard_map/ppermute | solution.py:40
  12.5 0.0 collective-permute-start.4
  12.5 0.0 copy-done.2
  12.5 0.5 %collective-permute-start.5 = (bf16[8,512]{1,0:T(8,128)(2,1)S(1)}, bf16[8,512]{1,0:T(8,128)(2,1)S(1)}, u32[]{:S(2)}, u32[]{:S(2)}) collective-permute-start(bf16[8,512]{1,0:T(8,128)(2,1)S(1)} %copy-done.2), channel_id=1, source_target_pairs={{0,1},{1,0},{2,3},{3,2},{4,5},{5,4},{6,7},{7,6},{8,9},{9,8},{10,11... | collective-permute-start | bytes 24584 | tf_op jit(solution)/shard_map/ppermute | solution.py:40
  13.0 0.6 %collective-permute-done.4.refs_9_.refs_10_ = s32[2,128]{1,0:T(2,128)S(1)} collective-permute-done((s32[2,128]{1,0:T(2,128)S(1)}, s32[2,128]{1,0:T(2,128)S(1)}, u32[]{:S(2)}, u32[]{:S(2)}) %collective-permute-start.4) | collective-permute-done | bytes 1056 | tf_op jit(solution)/shard_map/ppermute | solution.py:40
  13.7 0.0 copy-done.3
  13.7 0.2 collective-permute-start.6
  13.9 0.0 collective-permute-done.5.refs_10_.refs_11_
  13.9 1.0 %collective-permute-done.6.refs_11_.refs_12_ = bf16[8,512]{1,0:T(8,128)(2,1)S(1)} collective-permute-done((bf16[8,512]{1,0:T(8,128)(2,1)S(1)}, bf16[8,512]{1,0:T(8,128)(2,1)S(1)}, u32[]{:S(2)}, u32[]{:S(2)}) %collective-permute-start.6) | collective-permute-done | bytes 8224 | tf_op jit(solution)/shard_map/ppermute | solution.py:40
  14.9 0.0 collective-permute-done.7.refs_12_.refs_13_
  14.9 0.0 collective-permute-done.8.refs_13_.refs_14_
  14.9 0.0 copy-done
  14.9 0.0 copy-done.1
  14.9 1.3 %attend.2.refs_1_ = bf16[32,2176]{1,0:T(8,128)(2,1)S(1)} custom-call(bf16[32,2048]{1,0:T(8,128)(2,1)S(1)} %constant_dynamic-update-slice_fusion.refs_0_, f32[72,128]{1,0:T(8,128)S(1)} %get-tuple-element.17.refs_1_.refs_2_, f32[72,128]{1,0:T(8,128)S(1)} %get-tuple-element.18.refs_2_.refs_3_, s32[72,128]{1,0:T(8,128)S(1)} %get-tuple-element.19.refs_3_.refs_4_, ...), custom_call_target="tpu_custom_call" | custom-call | flops 201326592 | bytes 3407872 | tf_op jit(solution)/shard_map/attend/pallas_call | solution.py:228
  16.2 0.0 collective-permute-done.3.refs_0_
  16.3 1.4 %attend.3 = (bf16[16,2176]{1,0:T(8,128)(2,1)S(1)}, bf16[16,2176]{1,0:T(8,128)(2,1)S(1)}, bf16[16,2176]{1,0:T(8,128)(2,1)S(1)}, bf16[16,2176]{1,0:T(8,128)(2,1)S(1)}) custom-call(bf16[32,2048]{1,0:T(8,128)(2,1)S(1)} %collective-permute-done.3.refs_0_, bf16[32,2176]{1,0:T(8,128)(2,1)S(1)} %attend.2.refs_1_, f32[72,128]{1,0:T(8,128)S(1)} %get-tuple-element.17.refs_1_.refs_2_, ...), custom_call_target="tpu_custom_call" | custom-call | flops 201326592 | bytes 3407872 | tf_op jit(solution)/shard_map/attend/pallas_call | solution.py:228
  17.6 0.5 %collective-permute-start.9 = (bf16[16,2176]{1,0:T(8,128)(2,1)S(1)}, bf16[16,2176]{1,0:T(8,128)(2,1)S(1)}, u32[]{:S(2)}, u32[]{:S(2)}) collective-permute-start(bf16[16,2176]{1,0:T(8,128)(2,1)S(1)} %get-tuple-element.22), channel_id=1, source_target_pairs={{0,4},{1,5},{2,6},{3,7},{4,0},{5,1},{6,2},{7,3},{8,12},{9,13},{10,... | collective-permute-start | bytes 208904 | tf_op jit(solution)/shard_map/ppermute | solution.py:40
  18.1 1.4 %collective-permute-start.10 = (bf16[16,2176]{1,0:T(8,128)(2,1)S(1)}, bf16[16,2176]{1,0:T(8,128)(2,1)S(1)}, u32[]{:S(2)}, u32[]{:S(2)}) collective-permute-start(bf16[16,2176]{1,0:T(8,128)(2,1)S(1)} %get-tuple-element.23), channel_id=1, source_target_pairs={{0,8},{1,9},{2,10},{3,11},{4,12},{5,13},{6,14},{7,15},{8,0},{9,1},... | collective-permute-start | bytes 208904 | tf_op jit(solution)/shard_map/ppermute | solution.py:40
  19.5 2.6 %collective-permute-start.11 = (bf16[16,2176]{1,0:T(8,128)(2,1)S(1)}, bf16[16,2176]{1,0:T(8,128)(2,1)S(1)}, u32[]{:S(2)}, u32[]{:S(2)}) collective-permute-start(bf16[16,2176]{1,0:T(8,128)(2,1)S(1)} %get-tuple-element.24), channel_id=1, source_target_pairs={{0,12},{1,13},{2,14},{3,15},{4,8},{5,9},{6,10},{7,11},{8,4},{9,5},... | collective-permute-start | bytes 208904 | tf_op jit(solution)/shard_map/ppermute | solution.py:40
  22.1 0.7 %collective-permute-done.9.refs_1_ = bf16[16,2176]{1,0:T(8,128)(2,1)S(1)} collective-permute-done((bf16[16,2176]{1,0:T(8,128)(2,1)S(1)}, bf16[16,2176]{1,0:T(8,128)(2,1)S(1)}, u32[]{:S(2)}, u32[]{:S(2)}) %collective-permute-start.9) | collective-permute-done | bytes 69664 | tf_op jit(solution)/shard_map/ppermute | solution.py:40
  22.8 3.9 %collective-permute-done.10.refs_2_ = bf16[16,2176]{1,0:T(8,128)(2,1)S(1)} collective-permute-done((bf16[16,2176]{1,0:T(8,128)(2,1)S(1)}, bf16[16,2176]{1,0:T(8,128)(2,1)S(1)}, u32[]{:S(2)}, u32[]{:S(2)}) %collective-permute-start.10) | collective-permute-done | bytes 69664 | tf_op jit(solution)/shard_map/ppermute | solution.py:40
  26.7 0.0 collective-permute-done.11.refs_3_
  26.7 0.3 %merge.2 = (bf16[8,2176]{1,0:T(8,128)(2,1)S(1)}, bf16[8,2176]{1,0:T(8,128)(2,1)S(1)}) custom-call(bf16[16,2176]{1,0:T(8,128)(2,1)S(1)} %get-tuple-element.21.refs_0_, bf16[16,2176]{1,0:T(8,128)(2,1)S(1)} %collective-permute-done.9.refs_1_, bf16[16,2176]{1,0:T(8,128)(2,1)S(1)} %collective-permute-done.10.refs_2_, ...), custom_call_target="tpu_custom_call" | custom-call | flops 524288 | bytes 348160 | tf_op jit(solution)/shard_map/merge/pallas_call | solution.py:289
  27.1 0.6 %collective-permute-start.12 = (bf16[8,2176]{1,0:T(8,128)(2,1)S(1)}, bf16[8,2176]{1,0:T(8,128)(2,1)S(1)}, u32[]{:S(2)}, u32[]{:S(2)}) collective-permute-start(bf16[8,2176]{1,0:T(8,128)(2,1)S(1)} %get-tuple-element.26), channel_id=1, source_target_pairs={{0,2},{1,3},{2,0},{3,1},{4,6},{5,7},{6,4},{7,5},{8,10},{9,11},{10,... | collective-permute-start | bytes 104456 | tf_op jit(solution)/shard_map/ppermute | solution.py:40
  27.6 3.4 %collective-permute-done.12.refs_1_ = bf16[8,2176]{1,0:T(8,128)(2,1)S(1)} collective-permute-done((bf16[8,2176]{1,0:T(8,128)(2,1)S(1)}, bf16[8,2176]{1,0:T(8,128)(2,1)S(1)}, u32[]{:S(2)}, u32[]{:S(2)}) %collective-permute-start.12) | collective-permute-done | bytes 34848 | tf_op jit(solution)/shard_map/ppermute | solution.py:40
  31.1 0.9 %merge.3 = bf16[8,2048]{1,0:T(8,128)(2,1)} custom-call(bf16[8,2176]{1,0:T(8,128)(2,1)S(1)} %get-tuple-element.25.refs_0_, bf16[8,2176]{1,0:T(8,128)(2,1)S(1)} %collective-permute-done.12.refs_1_), custom_call_target="tpu_custom_call" | custom-call | flops 131072 | bytes 98304 | tf_op jit(solution)/shard_map/merge/pallas_call | solution.py:289
  (4 shorter events, 0.0 us)
Async XLA Ops:
  0.0 6.2 %copy-start.6 = (s32[2]{0:T(128)S(1)}, s32[2]{0:T(128)}, u32[]{:S(2)}) copy-start(s32[2]{0:T(128)} %start_ref.1) | copy-start | bytes 28
  0.0 6.2 %copy-start.5 = (s32[2,1]{0,1:T(1,128)S(1)}, s32[2,1]{0,1:T(1,128)}, u32[]{:S(2)}) copy-start(s32[2,1]{0,1:T(1,128)} %param.12) | copy-start | bytes 28
  0.0 7.7 %collective-permute-start = (bf16[8,2048]{1,0:T(8,128)(2,1)}, bf16[8,2048]{1,0:T(8,128)(2,1)S(1)}, u32[]{:S(2)}, u32[]{:S(2)}) collective-permute-start(bf16[8,2048]{1,0:T(8,128)(2,1)} %query_in.1), channel_id=1, source_target_pairs={{0,4},{1,5},{2,6},{3,7},{4,0},{5,1},{6,2},{7,3},{8,12},{9,13},{10,... | collective-permute-start | bytes 98312 | tf_op jit(solution)/shard_map/ppermute | solution.py:40
  3.1 7.9 %collective-permute-start.2 = (bf16[8,2048]{1,0:T(8,128)(2,1)}, bf16[8,2048]{1,0:T(8,128)(2,1)S(1)}, u32[]{:S(2)}, u32[]{:S(2)}) collective-permute-start(bf16[8,2048]{1,0:T(8,128)(2,1)} %query_in.1), channel_id=1, source_target_pairs={{0,12},{1,13},{2,14},{3,15},{4,8},{5,9},{6,10},{7,11},{8,4},{9,5},... | collective-permute-start | bytes 98312 | tf_op jit(solution)/shard_map/ppermute | solution.py:40
  5.5 5.4 %collective-permute-start.1 = (bf16[8,2048]{1,0:T(8,128)(2,1)}, bf16[8,2048]{1,0:T(8,128)(2,1)S(1)}, u32[]{:S(2)}, u32[]{:S(2)}) collective-permute-start(bf16[8,2048]{1,0:T(8,128)(2,1)} %query_in.1), channel_id=1, source_target_pairs={{0,8},{1,9},{2,10},{3,11},{4,12},{5,13},{6,14},{7,15},{8,0},{9,1},... | collective-permute-start | bytes 98312 | tf_op jit(solution)/shard_map/ppermute | solution.py:40
  5.7 9.2 %collective-permute-start.7 = (bf16[2,384,512]{2,1,0:T(8,128)(2,1)}, bf16[2,384,512]{2,1,0:T(8,128)(2,1)S(1)}, u32[]{:S(2)}, u32[]{:S(2)}) collective-permute-start(bf16[2,384,512]{2,1,0:T(8,128)(2,1)} %refs_8_.3), channel_id=1, source_target_pairs={{0,1},{1,0},{2,3},{3,2},{4,5},{5,4},{6,7},{7,6},{8,9},{9,8},{10,11... | collective-permute-start | bytes 2359304 | tf_op jit(solution)/shard_map/ppermute | solution.py:40
  5.7 9.2 %collective-permute-start.8 = (bf16[2,384,512]{2,1,0:T(8,128)(2,1)}, bf16[2,384,512]{2,1,0:T(8,128)(2,1)S(1)}, u32[]{:S(2)}, u32[]{:S(2)}) collective-permute-start(bf16[2,384,512]{2,1,0:T(8,128)(2,1)} %refs_9_.1), channel_id=1, source_target_pairs={{0,1},{1,0},{2,3},{3,2},{4,5},{5,4},{6,7},{7,6},{8,9},{9,8},{10,11... | collective-permute-start | bytes 2359304 | tf_op jit(solution)/shard_map/ppermute | solution.py:40
  6.2 0.8 %copy-start.4 = (bf16[8,2048]{1,0:T(8,128)(2,1)S(1)}, bf16[8,2048]{1,0:T(8,128)(2,1)}, u32[]{:S(2)}) copy-start(bf16[8,2048]{1,0:T(8,128)(2,1)} %query_in.1) | copy-start | bytes 98308
  6.9 7.9 %copy-start = (bf16[2,384,512]{2,1,0:T(8,128)(2,1)S(1)}, bf16[2,384,512]{2,1,0:T(8,128)(2,1)}, u32[]{:S(2)}) copy-start(bf16[2,384,512]{2,1,0:T(8,128)(2,1)} %refs_8_.3) | copy-start | bytes 2359300
  6.9 8.0 %copy-start.1 = (bf16[2,384,512]{2,1,0:T(8,128)(2,1)S(1)}, bf16[2,384,512]{2,1,0:T(8,128)(2,1)}, u32[]{:S(2)}) copy-start(bf16[2,384,512]{2,1,0:T(8,128)(2,1)} %refs_9_.1) | copy-start | bytes 2359300
  10.9 1.6 %copy-start.2 = (bf16[8,512]{1,0:T(8,128)(2,1)S(1)}, bf16[8,512]{1,0:T(8,128)(2,1)}, u32[]{:S(2)}) copy-start(bf16[8,512]{1,0:T(8,128)(2,1)} %refs_6_.3) | copy-start | bytes 24580
  10.9 2.8 %copy-start.3 = (bf16[8,512]{1,0:T(8,128)(2,1)S(1)}, bf16[8,512]{1,0:T(8,128)(2,1)}, u32[]{:S(2)}) copy-start(bf16[8,512]{1,0:T(8,128)(2,1)} %refs_7_.3) | copy-start | bytes 24580
  10.9 5.3 %collective-permute-start.3 = (bf16[32,2048]{1,0:T(8,128)(2,1)S(1)}, bf16[32,2048]{1,0:T(8,128)(2,1)S(1)}, u32[]{:S(2)}, u32[]{:S(2)}) collective-permute-start(bf16[32,2048]{1,0:T(8,128)(2,1)S(1)} %constant_dynamic-update-slice_fusion.refs_0_), channel_id=1, source_target_pairs={{0,2},{1,3},{2,0},{3,1},{4,6},{5,7},{6,4},{7,5},{8,10},{9,11},{10,... | collective-permute-start | bytes 393224 | tf_op jit(solution)/shard_map/ppermute | solution.py:40
  12.5 1.2 %collective-permute-start.4 = (s32[2,128]{1,0:T(2,128)S(1)}, s32[2,128]{1,0:T(2,128)S(1)}, u32[]{:S(2)}, u32[]{:S(2)}) collective-permute-start(s32[2,128]{1,0:T(2,128)S(1)} %get-tuple-element.20.refs_4_.refs_5_), channel_id=1, source_target_pairs={{0,1},{1,0},{2,3},{3,2},{4,5},{5,4},{6,7},{7,6},{8,9},{9,8},{10,11... | collective-permute-start | bytes 3080 | tf_op jit(solution)/shard_map/ppermute | solution.py:40
  12.5 1.3 %collective-permute-start.5 = (bf16[8,512]{1,0:T(8,128)(2,1)S(1)}, bf16[8,512]{1,0:T(8,128)(2,1)S(1)}, u32[]{:S(2)}, u32[]{:S(2)}) collective-permute-start(bf16[8,512]{1,0:T(8,128)(2,1)S(1)} %copy-done.2), channel_id=1, source_target_pairs={{0,1},{1,0},{2,3},{3,2},{4,5},{5,4},{6,7},{7,6},{8,9},{9,8},{10,11... | collective-permute-start | bytes 24584 | tf_op jit(solution)/shard_map/ppermute | solution.py:40
  13.7 1.2 %collective-permute-start.6 = (bf16[8,512]{1,0:T(8,128)(2,1)S(1)}, bf16[8,512]{1,0:T(8,128)(2,1)S(1)}, u32[]{:S(2)}, u32[]{:S(2)}) collective-permute-start(bf16[8,512]{1,0:T(8,128)(2,1)S(1)} %copy-done.3), channel_id=1, source_target_pairs={{0,1},{1,0},{2,3},{3,2},{4,5},{5,4},{6,7},{7,6},{8,9},{9,8},{10,11... | collective-permute-start | bytes 24584 | tf_op jit(solution)/shard_map/ppermute | solution.py:40
  17.6 5.2 %collective-permute-start.9 = (bf16[16,2176]{1,0:T(8,128)(2,1)S(1)}, bf16[16,2176]{1,0:T(8,128)(2,1)S(1)}, u32[]{:S(2)}, u32[]{:S(2)}) collective-permute-start(bf16[16,2176]{1,0:T(8,128)(2,1)S(1)} %get-tuple-element.22), channel_id=1, source_target_pairs={{0,4},{1,5},{2,6},{3,7},{4,0},{5,1},{6,2},{7,3},{8,12},{9,13},{10,... | collective-permute-start | bytes 208904 | tf_op jit(solution)/shard_map/ppermute | solution.py:40
  18.1 8.6 %collective-permute-start.10 = (bf16[16,2176]{1,0:T(8,128)(2,1)S(1)}, bf16[16,2176]{1,0:T(8,128)(2,1)S(1)}, u32[]{:S(2)}, u32[]{:S(2)}) collective-permute-start(bf16[16,2176]{1,0:T(8,128)(2,1)S(1)} %get-tuple-element.23), channel_id=1, source_target_pairs={{0,8},{1,9},{2,10},{3,11},{4,12},{5,13},{6,14},{7,15},{8,0},{9,1},... | collective-permute-start | bytes 208904 | tf_op jit(solution)/shard_map/ppermute | solution.py:40
  19.5 7.2 %collective-permute-start.11 = (bf16[16,2176]{1,0:T(8,128)(2,1)S(1)}, bf16[16,2176]{1,0:T(8,128)(2,1)S(1)}, u32[]{:S(2)}, u32[]{:S(2)}) collective-permute-start(bf16[16,2176]{1,0:T(8,128)(2,1)S(1)} %get-tuple-element.24), channel_id=1, source_target_pairs={{0,12},{1,13},{2,14},{3,15},{4,8},{5,9},{6,10},{7,11},{8,4},{9,5},... | collective-permute-start | bytes 208904 | tf_op jit(solution)/shard_map/ppermute | solution.py:40
  27.1 4.0 %collective-permute-start.12 = (bf16[8,2176]{1,0:T(8,128)(2,1)S(1)}, bf16[8,2176]{1,0:T(8,128)(2,1)S(1)}, u32[]{:S(2)}, u32[]{:S(2)}) collective-permute-start(bf16[8,2176]{1,0:T(8,128)(2,1)S(1)} %get-tuple-element.26), channel_id=1, source_target_pairs={{0,2},{1,3},{2,0},{3,1},{4,6},{5,7},{6,4},{7,5},{8,10},{9,11},{10,... | collective-permute-start | bytes 104456 | tf_op jit(solution)/shard_map/ppermute | solution.py:40

commit v2 on v1

v2 whole, which is shorter than its diff:
```python
import functools

import jax
import jax.numpy as jnp
import numpy as np
from jax import lax
from jax.experimental import pallas as pl
from jax.experimental.pallas import tpu as pltpu
from jax.sharding import PartitionSpec as P


HD = 128
LANES = 128
NEG_FILL = -1e30
MAX_FLOOR = -5e29
LOG2E = 1.4426950408889634
PREPARE_FLOPS = 10_000_000_000
BF = jnp.bfloat16
F32 = jnp.float32


def turn_table(head_size):
    half_size = head_size // 2
    frequency = 500000.0 ** (-np.arange(half_size) * 2.0 / head_size)
    turn_counts = np.floor(frequency / (2.0 * np.pi) * 2.0**32 + 0.5).astype(np.int64) % 2**32
    turn_counts = np.where(turn_counts >= 2**31, turn_counts - 2**32, turn_counts)
    return turn_counts.astype(np.int32)


def stages_of(devices):
    core = 2 if devices % 2 == 0 else 1
    rest = devices // core
    inner = 1 << ((rest.bit_length() - 1) // 2)
    outer = rest // inner
    return (core * inner, outer), (core, inner), (1, core)


def swap(values, distance):
    devices = lax.axis_size("kv")
    return lax.ppermute(values, "kv", [(i, i ^ distance) for i in range(devices)])


def rotate(values, cosine, signed_sine):
    return values * cosine + pltpu.roll(values, HD // 2, 1) * signed_sine


def split_pair(values):
    high = values.astype(BF).astype(F32)
    return high, (values - high).astype(BF).astype(F32)


def split_index(values, size):
    if size & (size - 1) == 0:
        return values >> (size.bit_length() - 1), values & (size - 1)
    quotient = lax.div(values, jnp.int32(size))
    return quotient, values - quotient * size


def prepare_kernel(share, span_len, stages, start_ref, query_in, query_out, cos_ref, sin_ref, offset_ref):
    (outer_stride, outer), (inner_stride, inner), (core_stride, _) = stages
    spans = start_ref.shape[0]
    me = lax.axis_index("kv")
    query_out[...] = query_in[...]
    lane = lax.broadcasted_iota(jnp.int32, (1, HD), 1)
    pair = jnp.where(lane < HD // 2, lane, lane - HD // 2)
    turns = jnp.zeros((1, HD), jnp.int32)
    for index, turn in enumerate(turn_table(HD)):
        turns = jnp.where(pair == index, jnp.int32(turn), turns)
    row = lax.broadcasted_iota(jnp.int32, cos_ref.shape, 0)
    member, within = split_index(row, share)
    high, low = split_index(member, inner)
    distance = jnp.where(high < outer, high * outer_stride + low * inner_stride, core_stride)
    token = (me ^ distance) * share + within
    span, step = split_index(token, span_len)
    start = jnp.full(cos_ref.shape, start_ref[0], jnp.int32)
    for index in range(1, spans):
        start = jnp.where(span == index, start_ref[index], start)
    angles = ((start + step) * turns).astype(F32) * (2.0 * np.pi / 2.0**32)
    cos_ref[...] = jnp.cos(angles)
    sine = jnp.sin(angles)
    sin_ref[...] = jnp.where(lane < HD // 2, -sine, sine)
    offset_ref[...] = token - me * share


def prepare(span_len, stages, starts, query_in):
    vmem = pl.BlockSpec(memory_space=pltpu.VMEM)
    smem = pl.BlockSpec(memory_space=pltpu.SMEM)
    share = query_in.shape[0]
    rows = share * (stages[0][1] * stages[1][1] + 1)
    table = jax.ShapeDtypeStruct((rows, HD), F32)
    whole = jax.ShapeDtypeStruct((rows, HD), jnp.int32)
    return pl.pallas_call(
        functools.partial(prepare_kernel, share, span_len, stages),
        out_shape=(jax.ShapeDtypeStruct(query_in.shape, BF), table, table, whole),
        in_specs=[smem, vmem],
        out_specs=(vmem,) * 4,
        cost_estimate=pl.CostEstimate(flops=PREPARE_FLOPS, bytes_accessed=12 * rows * HD, transcendentals=2 * rows * HD),
        compiler_params=pltpu.CompilerParams(vmem_limit_bytes=4 << 20),
        name="prepare",
    )(starts, query_in)


def attend_kernel(chunk, relative, core, core_stride, heads, kv_heads, span_len, *refs):
    (query_ref, cos_ref, sin_ref, offset_ref), refs = refs[:4], refs[4:]
    sides = [refs[side * 5 : side * 5 + 5] for side in range(core)]
    (out_ref,) = refs[5 * core :]
    share, slots = sides[0][1].shape[0], sides[0][3].shape[1]
    group = heads // kv_heads
    scale = HD**-0.5 * LOG2E
    rows = query_ref.shape[0]
    me = lax.axis_index("kv")
    own_span, _ = split_index(me * share, span_len)
    span = own_span ^ relative
    has_own = relative == 0
    key_rows = [slice(0, share), slice(cos_ref.shape[0] - share, cos_ref.shape[0])]
    nt = (((1,), (1,)), ((), ()))
    slot = lax.broadcasted_iota(jnp.int32, (1, slots), 1)
    biases = []
    for side in range(core):
        live = sides[side][0][...]
        here = lax.broadcasted_iota(jnp.int32, live.shape, 1) == span
        limit = jnp.sum(jnp.where(here, live, 0).astype(F32), axis=1, keepdims=True).astype(jnp.int32)
        biases.append(jnp.where(slot < limit, 0.0, NEG_FILL))
    lane = lax.broadcasted_iota(jnp.int32, (rows, LANES), 1)
    table = slice(chunk * rows, (chunk + 1) * rows)
    cos, sin = cos_ref[table, :], sin_ref[table, :]
    if has_own:
        other = ((me ^ core_stride) - me) * share - share
        place = jnp.where(lane < share, lane, lane + other)
        admitted = jnp.logical_and(place <= offset_ref[table, :], lane < core * share)
        own_bias = jnp.concatenate([jnp.where(admitted, 0.0, NEG_FILL)] * group, axis=0)

    def stack_new(blocks):
        filler = jnp.zeros((LANES - core * share, HD), F32)
        return jnp.concatenate([*blocks, filler], axis=0).astype(BF)

    raw = {}
    for g in range(kv_heads):
        stacked = []
        for h in range(g * group, (g + 1) * group):
            stacked.append(rotate(query_ref[:, h * HD : (h + 1) * HD].astype(F32), cos, sin))
        query = jnp.concatenate(stacked, axis=0).astype(BF)
        lanes = slice(g * HD, (g + 1) * HD)
        raw[g] = [
            lax.dot_general(query, sides[side][3][span, :, lanes], nt, preferred_element_type=F32)
            for side in range(core)
        ]
        if has_own:
            keys = stack_new(
                [
                    rotate(sides[side][1][:, lanes].astype(F32), cos_ref[key_rows[side], :], sin_ref[key_rows[side], :])
                    for side in range(core)
                ]
            )
            raw[g].append(lax.dot_general(query, keys, nt, preferred_element_type=F32))

    weights, columns = {}, {}
    for g in range(kv_heads):
        scores = [values * scale + bias for values, bias in zip(raw[g], biases + ([own_bias] if has_own else []))]
        top = functools.reduce(jnp.maximum, [jnp.max(values, axis=1, keepdims=True) for values in scores])
        top_high, top_low = split_pair(jnp.maximum(top, MAX_FLOOR))
        top = top_high + top_low
        found = [jnp.exp2(values - top) for values in scores]
        total = functools.reduce(jnp.add, [jnp.sum(values, axis=1, keepdims=True) for values in found])
        weights[g] = [values.astype(BF) for values in found]
        columns[g] = (top_high, top_low, *split_pair(total))

    for g in range(kv_heads):
        lanes = slice(g * HD, (g + 1) * HD)
        terms = [
            jnp.dot(weights[g][side], sides[side][4][span, :, lanes], preferred_element_type=F32) for side in range(core)
        ]
        if has_own:
            values = stack_new([sides[side][2][:, lanes].astype(F32) for side in range(core)])
            terms.append(jnp.dot(weights[g][core], values, preferred_element_type=F32))
        summed = functools.reduce(jnp.add, terms)
        for index in range(group):
            h = g * group + index
            out_ref[:, h * HD : (h + 1) * HD] = summed[index * rows : (index + 1) * rows].astype(BF)

    stats = jnp.zeros((rows, LANES), F32)
    for g in range(kv_heads):
        for index in range(group):
            own = slice(index * rows, (index + 1) * rows)
            for order, values in enumerate(columns[g]):
                stats = jnp.where(lane == order * heads + g * group + index, values[own], stats)
    out_ref[:, heads * HD :] = stats.astype(BF)


def attend(chunk, relative, stages, heads, kv_heads, span_len, query, tables, sides):
    vmem = pl.BlockSpec(memory_space=pltpu.VMEM)
    _, _, (core_stride, core) = stages
    rows, slots = query.shape[0], sides[0][3].shape[1]
    operands = [query, *tables, *[array for side in sides for array in side]]
    return pl.pallas_call(
        functools.partial(attend_kernel, chunk, relative, core, core_stride, heads, kv_heads, span_len),
        out_shape=jax.ShapeDtypeStruct((rows, heads * HD + LANES), BF),
        in_specs=[vmem] * len(operands),
        out_specs=vmem,
        cost_estimate=pl.CostEstimate(
            flops=4 * core * rows * heads * HD * slots,
            bytes_accessed=2 * core * sides[0][3].size + 4 * rows * heads * HD,
            transcendentals=core * rows * heads * slots,
        ),
        compiler_params=pltpu.CompilerParams(vmem_limit_bytes=8 << 20),
        name="attend",
    )(*operands)


def merge_kernel(groups, count, heads, last, *refs):
    outputs = refs[groups * count :]
    width = heads * HD
    sets = [refs[member * count : (member + 1) * count] for member in range(groups)]
    share = outputs[0].shape[0] // groups

    def store(member, lanes, values):
        for index, out in enumerate(outputs):
            out[member * share : (member + 1) * share, lanes] = values[index * share : (index + 1) * share].astype(BF)

    scaled = []
    for member, parts in enumerate(sets):
        pairs = []
        for part in parts:
            stats = part[:, width:].astype(F32)
            pairs.append(stats + pltpu.roll(stats, LANES - heads, 1))
        top = functools.reduce(jnp.maximum, pairs)
        factors = [jnp.exp2(own - top) for own in pairs]
        total = functools.reduce(
            jnp.add, [f * pltpu.roll(pair, LANES - 2 * heads, 1) for f, pair in zip(factors, pairs)]
        )
        if last:
            inverse = 1.0 / total
            factors = [f * inverse for f in factors]
        else:
            lane = lax.broadcasted_iota(jnp.int32, top.shape, 1)
            packed = jnp.zeros_like(top)
            for place, values in enumerate((*split_pair(top), *split_pair(total))):
                moved = pltpu.roll(values, place * heads, 1) if place else values
                packed = jnp.where(lane // heads == place, moved, packed)
            store(member, slice(width, width + LANES), packed)
        scaled.append(factors)
    for h in range(heads):
        lanes = slice(h * HD, (h + 1) * HD)
        for member, parts in enumerate(sets):
            terms = [f[:, h : h + 1] * part[:, lanes].astype(F32) for f, part in zip(scaled[member], parts)]
            store(member, lanes, functools.reduce(jnp.add, terms))


def merge(groups, pieces, heads, last=False):
    rows = groups[0][0].shape[0]
    count = len(groups[0])
    width = heads * HD + (0 if last else LANES)
    shape = jax.ShapeDtypeStruct((len(groups) * rows // pieces, width), BF)
    vmem = pl.BlockSpec(memory_space=pltpu.VMEM)
    total = len(groups) * count
    return pl.pallas_call(
        functools.partial(merge_kernel, len(groups), count, heads, last),
        out_shape=(shape,) * pieces,
        in_specs=[vmem] * total,
        out_specs=(vmem,) * pieces,
        cost_estimate=pl.CostEstimate(
            flops=4 * total * rows * heads * HD,
            bytes_accessed=2 * (total + len(groups)) * rows * width,
            transcendentals=total * rows * LANES,
        ),
        compiler_params=pltpu.CompilerParams(vmem_limit_bytes=4 << 20),
        name="merge",
    )(*[part for group in groups for part in group])


def per_device(query_in, key_in, value_in, cache_keys, cache_values, live_slots, span_starts):
    devices = lax.axis_size("kv")
    share = query_in.shape[0]
    span_count = span_starts.shape[0]
    span_len = share * devices // span_count
    heads = query_in.shape[1] // HD
    kv_heads = key_in.shape[1] // HD
    stages = stages_of(devices)
    (outer_stride, outer), (inner_stride, inner), (core_stride, core) = stages

    arrived = [swap(query_in, i * inner_stride) for i in range(1, inner)]
    other_keys = swap(cache_keys, core_stride)
    other_values = swap(cache_values, core_stride)
    small = (live_slots.reshape(1, span_count), key_in, value_in)
    other_small = [swap(array, core_stride) for array in small]
    query_own, *tables = prepare(span_len, stages, span_starts, query_in)
    rows = jnp.concatenate([query_own] + arrived, axis=0)
    sides = [(*small, cache_keys, cache_values), (*other_small, other_keys, other_values)]
    parts = []
    for k in range(outer):
        chunk = swap(rows, k * outer_stride) if k else rows
        part = attend(k, k * span_count // outer, stages, heads, kv_heads, span_len, chunk, tables, sides)
        parts.append(swap(part, k * outer_stride) if k else part)
    kept = merge([parts], inner, heads)
    received = [swap(kept[i], i * inner_stride) for i in range(1, inner)]
    (attended,) = merge([[kept[0]] + received], 1, heads, last=True)
    return attended


def solution(mesh):
    in_specs = (
        P(("groups", "kv"), None),
        P(("groups", "kv"), None),
        P(("groups", "kv"), None),
        P("groups", "kv", None),
        P("groups", "kv", None),
        P("groups", "kv"),
        P("groups"),
    )
    out_specs = P(("groups", "kv"), None)
    return jax.shard_map(per_device, mesh=mesh, in_specs=in_specs, out_specs=out_specs, check_vma=False)
```

time: 32.1 us -> 31.6 us (0.984)
  waiting for transfers between devices: 12.9 us -> 9.98 us
  starting transfers between devices: 13.4 us -> 14.7 us
  local copies, waits for them, and re-layouts: 0.8 us -> 1.45 us
  Pallas kernels: 4.66 us -> 5.19 us
    ppermute x13, waiting for transfers between devices: 12.9 us -> 9.98 us  [swap(): lax.ppermute(values, 'kv', [(i, i ^ distance) for i in range(devices)])]
    ppermute x13, starting transfers between devices: 13.4 us -> 14.7 us  [swap(): lax.ppermute(values, 'kv', [(i, i ^ distance) for i in range(devices)])]
    unnamed x17 -> x15, local copies, waits for them, and re-layouts: 0.79 us -> 1.44 us
    pallas_call x2 -> x4, Pallas kernels: 2.72 us -> 3.25 us  [attend(): pl.pallas_call(functools.partial(attend_kernel, chunk, relative, core, co...]
  transfers between devices with their start and end apart: 13 -> 13, of which waited for: 6 -> 7; matrix products, arithmetic and copies ran while one was open for 0% -> 0% of each run, Pallas kernels for 7% -> 13%
where the time goes in v2:
time: 31.6 us; the launch traced here: 31.4 us
  starting transfers between devices  14.7 us (47%)
  waiting for transfers between devices  9.98 us (32%)
  Pallas kernels  5.19 us (16%)
  local copies, waits for them, and re-layouts  1.45 us (5%)
    ppermute x13, starting transfers between devices, swap(): lax.ppermute(values, 'kv', [(i, i ^ distance) for i in range(devices)])  14.7 us
    ppermute x13, waiting for transfers between devices, swap(): lax.ppermute(values, 'kv', [(i, i ^ distance) for i in range(devices)])  9.98 us
    pallas_call x4, Pallas kernels, attend(): pl.pallas_call(functools.partial(attend_kernel, chunk, relative, core, co...  3.25 us
    unnamed x15, local copies, waits for them, and re-layouts  1.44 us
    pallas_call x2, Pallas kernels, merge(): pl.pallas_call(functools.partial(merge_kernel, len(groups), count, heads,...  1.2 us
    pallas_call x1, Pallas kernels, prepare(): pl.pallas_call(functools.partial(prepare_kernel, share, span_len, stages)...  0.74 us
  transfers between devices with their start and end apart: 13, of which 7 were waited for; matrix products, arithmetic and copies ran while one was open for 0% of the time, Pallas kernels for 13%

profile of v2, /device:TPU:0, one launch (start us, length us, event | category | flops | bytes accessed | tf_op | source)
XLA Modules:
  0.0 31.4 jit_solution(11468494460797091397)
XLA Ops:
  0.0 0.0 copy-start
  0.0 0.0 copy-start.1
  0.0 3.0 %collective-permute-start = (bf16[8,2048]{1,0:T(8,128)(2,1)}, bf16[8,2048]{1,0:T(8,128)(2,1)S(1)}, u32[]{:S(2)}, u32[]{:S(2)}) collective-permute-start(bf16[8,2048]{1,0:T(8,128)(2,1)} %query_in.1), channel_id=1, source_target_pairs={{0,2},{1,3},{2,0},{3,1},{4,6},{5,7},{6,4},{7,5},{8,10},{9,11},{10,... | collective-permute-start | bytes 98312 | tf_op jit(solution)/shard_map/ppermute | solution.py:40
  3.0 0.0 collective-permute-start.4
  3.0 0.5 %collective-permute-start.5 = (bf16[2,384,512]{2,1,0:T(8,128)(2,1)}, bf16[2,384,512]{2,1,0:T(8,128)(2,1)S(1)}, u32[]{:S(2)}, u32[]{:S(2)}) collective-permute-start(bf16[2,384,512]{2,1,0:T(8,128)(2,1)} %refs_8_.7), channel_id=1, source_target_pairs={{0,1},{1,0},{2,3},{3,2},{4,5},{5,4},{6,7},{7,6},{8,9},{9,8},{10,11... | collective-permute-start | bytes 2359304 | tf_op jit(solution)/shard_map/ppermute | solution.py:40
  3.5 0.0 copy-start.5
  3.5 0.8 %copy-done.5 = bf16[8,2048]{1,0:T(8,128)(2,1)S(1)} copy-done((bf16[8,2048]{1,0:T(8,128)(2,1)S(1)}, bf16[8,2048]{1,0:T(8,128)(2,1)}, u32[]{:S(2)}) %copy-start.5) | copy-done | bytes 32792
  4.3 0.0 copy-start.6
  4.3 0.7 %copy-done.6 = s32[2]{0:T(128)S(1)} copy-done((s32[2]{0:T(128)S(1)}, s32[2]{0:T(128)}, u32[]{:S(2)}) %copy-start.6) | copy-done | bytes 32
  4.9 0.7 %prepare.1 = (bf16[8,2048]{1,0:T(8,128)(2,1)S(1)}, f32[72,128]{1,0:T(8,128)S(1)}, f32[72,128]{1,0:T(8,128)S(1)}, s32[72,128]{1,0:T(8,128)S(1)}) custom-call(s32[2]{0:T(128)S(1)} %copy-done.6, bf16[8,2048]{1,0:T(8,128)(2,1)S(1)} %copy-done.5), custom_call_target="tpu_custom_call" | custom-call | flops 10000000000 | bytes 110592 | tf_op jit(solution)/shard_map/prepare/pallas_call | solution.py:92
  5.7 0.0 copy-start.2
  5.7 0.0 copy-start.3
  5.7 0.0 collective-permute-done
  5.7 0.0 copy-start.4
  5.7 1.6 %collective-permute-start.6 = (bf16[16,2048]{1,0:T(8,128)(2,1)S(1)}, bf16[16,2048]{1,0:T(8,128)(2,1)S(1)}, u32[]{:S(2)}, u32[]{:S(2)}) collective-permute-start(bf16[16,2048]{1,0:T(8,128)(2,1)S(1)} %constant_dynamic-update-slice_fusion.refs_0_), channel_id=1, source_target_pairs={{0,4},{1,5},{2,6},{3,7},{4,0},{5,1},{6,2},{7,3},{8,12},{9,13},{10,... | collective-permute-start | bytes 196616 | tf_op jit(solution)/shard_map/ppermute | solution.py:40
  7.4 0.0 copy-done.2
  7.4 0.0 collective-permute-start.2
  7.4 0.0 copy-done.4
  7.4 0.5 %collective-permute-start.1 = (s32[1,2]{1,0:T(1,128)S(1)}, s32[1,2]{1,0:T(1,128)S(1)}, u32[]{:S(2)}, u32[]{:S(2)}) collective-permute-start(s32[1,2]{1,0:T(1,128)S(1)} %bitcast.1), channel_id=1, source_target_pairs={{0,1},{1,0},{2,3},{3,2},{4,5},{5,4},{6,7},{7,6},{8,9},{9,8},{10,11... | collective-permute-start | bytes 32 | tf_op jit(solution)/shard_map/ppermute | solution.py:40
  7.9 0.8 %collective-permute-done.1.refs_9_ = s32[1,2]{1,0:T(1,128)S(1)} collective-permute-done((s32[1,2]{1,0:T(1,128)S(1)}, s32[1,2]{1,0:T(1,128)S(1)}, u32[]{:S(2)}, u32[]{:S(2)}) %collective-permute-start.1) | collective-permute-done | bytes 40 | tf_op jit(solution)/shard_map/ppermute | solution.py:40
  8.7 2.6 %collective-permute-start.8 = (bf16[16,2048]{1,0:T(8,128)(2,1)S(1)}, bf16[16,2048]{1,0:T(8,128)(2,1)S(1)}, u32[]{:S(2)}, u32[]{:S(2)}) collective-permute-start(bf16[16,2048]{1,0:T(8,128)(2,1)S(1)} %constant_dynamic-update-slice_fusion.refs_0_), channel_id=1, source_target_pairs={{0,8},{1,9},{2,10},{3,11},{4,12},{5,13},{6,14},{7,15},{8,0},{9,1},... | collective-permute-start | bytes 196616 | tf_op jit(solution)/shard_map/ppermute | solution.py:40
  11.3 0.0 collective-permute-done.2.refs_10_
  11.3 0.0 copy-done.3
  11.3 0.1 collective-permute-start.3
  11.4 1.1 %collective-permute-done.3.refs_11_ = bf16[8,512]{1,0:T(8,128)(2,1)S(1)} collective-permute-done((bf16[8,512]{1,0:T(8,128)(2,1)S(1)}, bf16[8,512]{1,0:T(8,128)(2,1)S(1)}, u32[]{:S(2)}, u32[]{:S(2)}) %collective-permute-start.3) | collective-permute-done | bytes 8224 | tf_op jit(solution)/shard_map/ppermute | solution.py:40
  12.5 0.3 %collective-permute-start.10 = (bf16[16,2048]{1,0:T(8,128)(2,1)S(1)}, bf16[16,2048]{1,0:T(8,128)(2,1)S(1)}, u32[]{:S(2)}, u32[]{:S(2)}) collective-permute-start(bf16[16,2048]{1,0:T(8,128)(2,1)S(1)} %constant_dynamic-update-slice_fusion.refs_0_), channel_id=1, source_target_pairs={{0,12},{1,13},{2,14},{3,15},{4,8},{5,9},{6,10},{7,11},{8,4},{9,5},... | collective-permute-start | bytes 196616 | tf_op jit(solution)/shard_map/ppermute | solution.py:40
  12.8 0.0 collective-permute-done.6.refs_0_
  12.8 0.0 collective-permute-done.4.refs_12_
  12.8 0.0 collective-permute-done.5.refs_13_
  12.8 0.0 copy-done
  12.9 0.0 copy-done.1
  12.9 0.8 %attend.5 = bf16[16,2176]{1,0:T(8,128)(2,1)S(1)} custom-call(bf16[16,2048]{1,0:T(8,128)(2,1)S(1)} %collective-permute-done.6.refs_0_, f32[72,128]{1,0:T(8,128)S(1)} %get-tuple-element.12.refs_1_, f32[72,128]{1,0:T(8,128)S(1)} %get-tuple-element.13.refs_2_, s32[72,128]{1,0:T(8,128)S(1)} %get-tuple-element.14.refs_3_, s32[1,2]{1,0:T(1,128)S(1)} %bitcast.2, ...), custom_call_target="tpu_custom_call" | custom-call | flops 100663296 | bytes 1703936 | tf_op jit(solution)/shard_map/attend/pallas_call | solution.py:195
  13.7 0.6 %collective-permute-start.7 = (bf16[16,2176]{1,0:T(8,128)(2,1)S(1)}, bf16[16,2176]{1,0:T(8,128)(2,1)S(1)}, u32[]{:S(2)}, u32[]{:S(2)}) collective-permute-start(bf16[16,2176]{1,0:T(8,128)(2,1)S(1)} %attend.5), channel_id=1, source_target_pairs={{0,4},{1,5},{2,6},{3,7},{4,0},{5,1},{6,2},{7,3},{8,12},{9,13},{10,... | collective-permute-start | bytes 208904 | tf_op jit(solution)/shard_map/ppermute | solution.py:40
  14.3 1.1 %collective-permute-done.8.refs_0_ = bf16[16,2048]{1,0:T(8,128)(2,1)S(1)} collective-permute-done((bf16[16,2048]{1,0:T(8,128)(2,1)S(1)}, bf16[16,2048]{1,0:T(8,128)(2,1)S(1)}, u32[]{:S(2)}, u32[]{:S(2)}) %collective-permute-start.8) | collective-permute-done | bytes 65568 | tf_op jit(solution)/shard_map/ppermute | solution.py:40
  15.5 0.8 %attend.6 = bf16[16,2176]{1,0:T(8,128)(2,1)S(1)} custom-call(bf16[16,2048]{1,0:T(8,128)(2,1)S(1)} %collective-permute-done.8.refs_0_, f32[72,128]{1,0:T(8,128)S(1)} %get-tuple-element.12.refs_1_, f32[72,128]{1,0:T(8,128)S(1)} %get-tuple-element.13.refs_2_, s32[72,128]{1,0:T(8,128)S(1)} %get-tuple-element.14.refs_3_, s32[1,2]{1,0:T(1,128)S(1)} %bitcast.3, ...), custom_call_target="tpu_custom_call" | custom-call | flops 100663296 | bytes 1703936 | tf_op jit(solution)/shard_map/attend/pallas_call | solution.py:195
  16.3 2.4 %collective-permute-start.9 = (bf16[16,2176]{1,0:T(8,128)(2,1)S(1)}, bf16[16,2176]{1,0:T(8,128)(2,1)S(1)}, u32[]{:S(2)}, u32[]{:S(2)}) collective-permute-start(bf16[16,2176]{1,0:T(8,128)(2,1)S(1)} %attend.6), channel_id=1, source_target_pairs={{0,8},{1,9},{2,10},{3,11},{4,12},{5,13},{6,14},{7,15},{8,0},{9,1},... | collective-permute-start | bytes 208904 | tf_op jit(solution)/shard_map/ppermute | solution.py:40
  18.7 0.4 %collective-permute-done.10.refs_0_ = bf16[16,2048]{1,0:T(8,128)(2,1)S(1)} collective-permute-done((bf16[16,2048]{1,0:T(8,128)(2,1)S(1)}, bf16[16,2048]{1,0:T(8,128)(2,1)S(1)}, u32[]{:S(2)}, u32[]{:S(2)}) %collective-permute-start.10) | collective-permute-done | bytes 65568 | tf_op jit(solution)/shard_map/ppermute | solution.py:40
  19.1 0.8 %attend.7 = bf16[16,2176]{1,0:T(8,128)(2,1)S(1)} custom-call(bf16[16,2048]{1,0:T(8,128)(2,1)S(1)} %collective-permute-done.10.refs_0_, f32[72,128]{1,0:T(8,128)S(1)} %get-tuple-element.12.refs_1_, f32[72,128]{1,0:T(8,128)S(1)} %get-tuple-element.13.refs_2_, s32[72,128]{1,0:T(8,128)S(1)} %get-tuple-element.14.refs_3_, s32[1,2]{1,0:T(1,128)S(1)} %bitcast.4, ...), custom_call_target="tpu_custom_call" | custom-call | flops 100663296 | bytes 1703936 | tf_op jit(solution)/shard_map/attend/pallas_call | solution.py:195
  19.9 1.6 %collective-permute-start.11 = (bf16[16,2176]{1,0:T(8,128)(2,1)S(1)}, bf16[16,2176]{1,0:T(8,128)(2,1)S(1)}, u32[]{:S(2)}, u32[]{:S(2)}) collective-permute-start(bf16[16,2176]{1,0:T(8,128)(2,1)S(1)} %attend.7), channel_id=1, source_target_pairs={{0,12},{1,13},{2,14},{3,15},{4,8},{5,9},{6,10},{7,11},{8,4},{9,5},... | collective-permute-start | bytes 208904 | tf_op jit(solution)/shard_map/ppermute | solution.py:40
  21.5 0.8 %attend.4.refs_0_ = bf16[16,2176]{1,0:T(8,128)(2,1)S(1)} custom-call(bf16[16,2048]{1,0:T(8,128)(2,1)S(1)} %constant_dynamic-update-slice_fusion.refs_0_, f32[72,128]{1,0:T(8,128)S(1)} %get-tuple-element.12.refs_1_, f32[72,128]{1,0:T(8,128)S(1)} %get-tuple-element.13.refs_2_, s32[72,128]{1,0:T(8,128)S(1)} %get-tuple-element.14.refs_3_, s32[1,2]{1,0:T(1,128)S(1)} %bitcast.5, ...), custom_call_target="tpu_custom_call" | custom-call | flops 100663296 | bytes 1703936 | tf_op jit(solution)/shard_map/attend/pallas_call | solution.py:195
  22.4 0.0 collective-permute-done.7.refs_1_
  22.4 0.8 %collective-permute-done.9.refs_2_ = bf16[16,2176]{1,0:T(8,128)(2,1)S(1)} collective-permute-done((bf16[16,2176]{1,0:T(8,128)(2,1)S(1)}, bf16[16,2176]{1,0:T(8,128)(2,1)S(1)}, u32[]{:S(2)}, u32[]{:S(2)}) %collective-permute-start.9) | collective-permute-done | bytes 69664 | tf_op jit(solution)/shard_map/ppermute | solution.py:40
  23.1 3.1 %collective-permute-done.11.refs_3_ = bf16[16,2176]{1,0:T(8,128)(2,1)S(1)} collective-permute-done((bf16[16,2176]{1,0:T(8,128)(2,1)S(1)}, bf16[16,2176]{1,0:T(8,128)(2,1)S(1)}, u32[]{:S(2)}, u32[]{:S(2)}) %collective-permute-start.11) | collective-permute-done | bytes 69664 | tf_op jit(solution)/shard_map/ppermute | solution.py:40
  26.2 0.3 %merge.2 = (bf16[8,2176]{1,0:T(8,128)(2,1)S(1)}, bf16[8,2176]{1,0:T(8,128)(2,1)S(1)}) custom-call(bf16[16,2176]{1,0:T(8,128)(2,1)S(1)} %attend.4.refs_0_, bf16[16,2176]{1,0:T(8,128)(2,1)S(1)} %collective-permute-done.7.refs_1_, bf16[16,2176]{1,0:T(8,128)(2,1)S(1)} %collective-permute-done.9.refs_2_, bf16[16,2176]{1,0:T(8,128)(2,1)S(1)} %collective-permute-done.11.refs_3_), custom_call_target="tpu_custom_call" | custom-call | flops 524288 | bytes 348160 | tf_op jit(solution)/shard_map/merge/pallas_call | solution.py:256
  26.5 1.4 %collective-permute-start.12 = (bf16[8,2176]{1,0:T(8,128)(2,1)S(1)}, bf16[8,2176]{1,0:T(8,128)(2,1)S(1)}, u32[]{:S(2)}, u32[]{:S(2)}) collective-permute-start(bf16[8,2176]{1,0:T(8,128)(2,1)S(1)} %get-tuple-element.16), channel_id=1, source_target_pairs={{0,2},{1,3},{2,0},{3,1},{4,6},{5,7},{6,4},{7,5},{8,10},{9,11},{10,... | collective-permute-start | bytes 104456 | tf_op jit(solution)/shard_map/ppermute | solution.py:40
  27.9 2.6 %collective-permute-done.12.refs_1_ = bf16[8,2176]{1,0:T(8,128)(2,1)S(1)} collective-permute-done((bf16[8,2176]{1,0:T(8,128)(2,1)S(1)}, bf16[8,2176]{1,0:T(8,128)(2,1)S(1)}, u32[]{:S(2)}, u32[]{:S(2)}) %collective-permute-start.12) | collective-permute-done | bytes 34848 | tf_op jit(solution)/shard_map/ppermute | solution.py:40
  30.5 0.9 %merge.3 = bf16[8,2048]{1,0:T(8,128)(2,1)} custom-call(bf16[8,2176]{1,0:T(8,128)(2,1)S(1)} %get-tuple-element.15.refs_0_, bf16[8,2176]{1,0:T(8,128)(2,1)S(1)} %collective-permute-done.12.refs_1_), custom_call_target="tpu_custom_call" | custom-call | flops 131072 | bytes 98304 | tf_op jit(solution)/shard_map/merge/pallas_call | solution.py:256
  (2 shorter events, 0.0 us)
Async XLA Ops:
  0.0 12.8 %copy-start = (bf16[2,384,512]{2,1,0:T(8,128)(2,1)S(1)}, bf16[2,384,512]{2,1,0:T(8,128)(2,1)}, u32[]{:S(2)}) copy-start(bf16[2,384,512]{2,1,0:T(8,128)(2,1)} %refs_7_.7) | copy-start | bytes 2359300
  0.0 12.9 %copy-start.1 = (bf16[2,384,512]{2,1,0:T(8,128)(2,1)S(1)}, bf16[2,384,512]{2,1,0:T(8,128)(2,1)}, u32[]{:S(2)}) copy-start(bf16[2,384,512]{2,1,0:T(8,128)(2,1)} %refs_8_.7) | copy-start | bytes 2359300
  0.0 5.7 %collective-permute-start = (bf16[8,2048]{1,0:T(8,128)(2,1)}, bf16[8,2048]{1,0:T(8,128)(2,1)S(1)}, u32[]{:S(2)}, u32[]{:S(2)}) collective-permute-start(bf16[8,2048]{1,0:T(8,128)(2,1)} %query_in.1), channel_id=1, source_target_pairs={{0,2},{1,3},{2,0},{3,1},{4,6},{5,7},{6,4},{7,5},{8,10},{9,11},{10,... | collective-permute-start | bytes 98312 | tf_op jit(solution)/shard_map/ppermute | solution.py:40
  3.0 9.8 %collective-permute-start.4 = (bf16[2,384,512]{2,1,0:T(8,128)(2,1)}, bf16[2,384,512]{2,1,0:T(8,128)(2,1)S(1)}, u32[]{:S(2)}, u32[]{:S(2)}) collective-permute-start(bf16[2,384,512]{2,1,0:T(8,128)(2,1)} %refs_7_.7), channel_id=1, source_target_pairs={{0,1},{1,0},{2,3},{3,2},{4,5},{5,4},{6,7},{7,6},{8,9},{9,8},{10,11... | collective-permute-start | bytes 2359304 | tf_op jit(solution)/shard_map/ppermute | solution.py:40
  3.0 9.8 %collective-permute-start.5 = (bf16[2,384,512]{2,1,0:T(8,128)(2,1)}, bf16[2,384,512]{2,1,0:T(8,128)(2,1)S(1)}, u32[]{:S(2)}, u32[]{:S(2)}) collective-permute-start(bf16[2,384,512]{2,1,0:T(8,128)(2,1)} %refs_8_.7), channel_id=1, source_target_pairs={{0,1},{1,0},{2,3},{3,2},{4,5},{5,4},{6,7},{7,6},{8,9},{9,8},{10,11... | collective-permute-start | bytes 2359304 | tf_op jit(solution)/shard_map/ppermute | solution.py:40
  3.5 0.8 %copy-start.5 = (bf16[8,2048]{1,0:T(8,128)(2,1)S(1)}, bf16[8,2048]{1,0:T(8,128)(2,1)}, u32[]{:S(2)}) copy-start(bf16[8,2048]{1,0:T(8,128)(2,1)} %query_in.1) | copy-start | bytes 98308
  4.3 0.7 %copy-start.6 = (s32[2]{0:T(128)S(1)}, s32[2]{0:T(128)}, u32[]{:S(2)}) copy-start(s32[2]{0:T(128)} %start_ref.1) | copy-start | bytes 28
  5.7 1.7 %copy-start.2 = (bf16[8,512]{1,0:T(8,128)(2,1)S(1)}, bf16[8,512]{1,0:T(8,128)(2,1)}, u32[]{:S(2)}) copy-start(bf16[8,512]{1,0:T(8,128)(2,1)} %refs_5_.7) | copy-start | bytes 24580
  5.7 5.6 %copy-start.3 = (bf16[8,512]{1,0:T(8,128)(2,1)S(1)}, bf16[8,512]{1,0:T(8,128)(2,1)}, u32[]{:S(2)}) copy-start(bf16[8,512]{1,0:T(8,128)(2,1)} %refs_6_.7) | copy-start | bytes 24580
  5.7 1.7 %copy-start.4 = (s32[2,1]{0,1:T(1,128)S(1)}, s32[2,1]{0,1:T(1,128)}, u32[]{:S(2)}) copy-start(s32[2,1]{0,1:T(1,128)} %param.12) | copy-start | bytes 28
  5.7 7.1 %collective-permute-start.6 = (bf16[16,2048]{1,0:T(8,128)(2,1)S(1)}, bf16[16,2048]{1,0:T(8,128)(2,1)S(1)}, u32[]{:S(2)}, u32[]{:S(2)}) collective-permute-start(bf16[16,2048]{1,0:T(8,128)(2,1)S(1)} %constant_dynamic-update-slice_fusion.refs_0_), channel_id=1, source_target_pairs={{0,4},{1,5},{2,6},{3,7},{4,0},{5,1},{6,2},{7,3},{8,12},{9,13},{10,... | collective-permute-start | bytes 196616 | tf_op jit(solution)/shard_map/ppermute | solution.py:40
  7.4 3.9 %collective-permute-start.2 = (bf16[8,512]{1,0:T(8,128)(2,1)S(1)}, bf16[8,512]{1,0:T(8,128)(2,1)S(1)}, u32[]{:S(2)}, u32[]{:S(2)}) collective-permute-start(bf16[8,512]{1,0:T(8,128)(2,1)S(1)} %copy-done.2), channel_id=1, source_target_pairs={{0,1},{1,0},{2,3},{3,2},{4,5},{5,4},{6,7},{7,6},{8,9},{9,8},{10,11... | collective-permute-start | bytes 24584 | tf_op jit(solution)/shard_map/ppermute | solution.py:40
  7.4 1.3 %collective-permute-start.1 = (s32[1,2]{1,0:T(1,128)S(1)}, s32[1,2]{1,0:T(1,128)S(1)}, u32[]{:S(2)}, u32[]{:S(2)}) collective-permute-start(s32[1,2]{1,0:T(1,128)S(1)} %bitcast.1), channel_id=1, source_target_pairs={{0,1},{1,0},{2,3},{3,2},{4,5},{5,4},{6,7},{7,6},{8,9},{9,8},{10,11... | collective-permute-start | bytes 32 | tf_op jit(solution)/shard_map/ppermute | solution.py:40
  8.7 6.7 %collective-permute-start.8 = (bf16[16,2048]{1,0:T(8,128)(2,1)S(1)}, bf16[16,2048]{1,0:T(8,128)(2,1)S(1)}, u32[]{:S(2)}, u32[]{:S(2)}) collective-permute-start(bf16[16,2048]{1,0:T(8,128)(2,1)S(1)} %constant_dynamic-update-slice_fusion.refs_0_), channel_id=1, source_target_pairs={{0,8},{1,9},{2,10},{3,11},{4,12},{5,13},{6,14},{7,15},{8,0},{9,1},... | collective-permute-start | bytes 196616 | tf_op jit(solution)/shard_map/ppermute | solution.py:40
  11.3 1.2 %collective-permute-start.3 = (bf16[8,512]{1,0:T(8,128)(2,1)S(1)}, bf16[8,512]{1,0:T(8,128)(2,1)S(1)}, u32[]{:S(2)}, u32[]{:S(2)}) collective-permute-start(bf16[8,512]{1,0:T(8,128)(2,1)S(1)} %copy-done.3), channel_id=1, source_target_pairs={{0,1},{1,0},{2,3},{3,2},{4,5},{5,4},{6,7},{7,6},{8,9},{9,8},{10,11... | collective-permute-start | bytes 24584 | tf_op jit(solution)/shard_map/ppermute | solution.py:40
  12.5 6.6 %collective-permute-start.10 = (bf16[16,2048]{1,0:T(8,128)(2,1)S(1)}, bf16[16,2048]{1,0:T(8,128)(2,1)S(1)}, u32[]{:S(2)}, u32[]{:S(2)}) collective-permute-start(bf16[16,2048]{1,0:T(8,128)(2,1)S(1)} %constant_dynamic-update-slice_fusion.refs_0_), channel_id=1, source_target_pairs={{0,12},{1,13},{2,14},{3,15},{4,8},{5,9},{6,10},{7,11},{8,4},{9,5},... | collective-permute-start | bytes 196616 | tf_op jit(solution)/shard_map/ppermute | solution.py:40
  13.7 8.7 %collective-permute-start.7 = (bf16[16,2176]{1,0:T(8,128)(2,1)S(1)}, bf16[16,2176]{1,0:T(8,128)(2,1)S(1)}, u32[]{:S(2)}, u32[]{:S(2)}) collective-permute-start(bf16[16,2176]{1,0:T(8,128)(2,1)S(1)} %attend.5), channel_id=1, source_target_pairs={{0,4},{1,5},{2,6},{3,7},{4,0},{5,1},{6,2},{7,3},{8,12},{9,13},{10,... | collective-permute-start | bytes 208904 | tf_op jit(solution)/shard_map/ppermute | solution.py:40
  16.3 6.9 %collective-permute-start.9 = (bf16[16,2176]{1,0:T(8,128)(2,1)S(1)}, bf16[16,2176]{1,0:T(8,128)(2,1)S(1)}, u32[]{:S(2)}, u32[]{:S(2)}) collective-permute-start(bf16[16,2176]{1,0:T(8,128)(2,1)S(1)} %attend.6), channel_id=1, source_target_pairs={{0,8},{1,9},{2,10},{3,11},{4,12},{5,13},{6,14},{7,15},{8,0},{9,1},... | collective-permute-start | bytes 208904 | tf_op jit(solution)/shard_map/ppermute | solution.py:40
  19.9 6.3 %collective-permute-start.11 = (bf16[16,2176]{1,0:T(8,128)(2,1)S(1)}, bf16[16,2176]{1,0:T(8,128)(2,1)S(1)}, u32[]{:S(2)}, u32[]{:S(2)}) collective-permute-start(bf16[16,2176]{1,0:T(8,128)(2,1)S(1)} %attend.7), channel_id=1, source_target_pairs={{0,12},{1,13},{2,14},{3,15},{4,8},{5,9},{6,10},{7,11},{8,4},{9,5},... | collective-permute-start | bytes 208904 | tf_op jit(solution)/shard_map/ppermute | solution.py:40
  26.5 4.0 %collective-permute-start.12 = (bf16[8,2176]{1,0:T(8,128)(2,1)S(1)}, bf16[8,2176]{1,0:T(8,128)(2,1)S(1)}, u32[]{:S(2)}, u32[]{:S(2)}) collective-permute-start(bf16[8,2176]{1,0:T(8,128)(2,1)S(1)} %get-tuple-element.16), channel_id=1, source_target_pairs={{0,2},{1,3},{2,0},{3,1},{4,6},{5,7},{6,4},{7,5},{8,10},{9,11},{10,... | collective-permute-start | bytes 104456 | tf_op jit(solution)/shard_map/ppermute | solution.py:40

commit v3 on v2

--- a/solution.py
+++ b/solution.py
@@ -103,7 +103,8 @@
 def attend_kernel(chunk, relative, core, core_stride, heads, kv_heads, span_len, *refs):
     (query_ref, cos_ref, sin_ref, offset_ref), refs = refs[:4], refs[4:]
     sides = [refs[side * 5 : side * 5 + 5] for side in range(core)]
-    (out_ref,) = refs[5 * core :]
+    outputs = refs[5 * core :]
+    piece = outputs[0].shape[0]
     share, slots = sides[0][1].shape[0], sides[0][3].shape[1]
     group = heads // kv_heads
     scale = HD**-0.5 * LOG2E
@@ -176,15 +177,23 @@
         summed = functools.reduce(jnp.add, terms)
         for index in range(group):
             h = g * group + index
-            out_ref[:, h * HD : (h + 1) * HD] = summed[index * rows : (index + 1) * rows].astype(BF)
-
-    stats = jnp.zeros((rows, LANES), F32)
+            for n, out in enumerate(outputs):
+                at = index * rows + n * piece
+                out[:, h * HD : (h + 1) * HD] = summed[at : at + piece].astype(BF)
+
+    head, place = lane % heads, lane // heads
+    stats = []
     for g in range(kv_heads):
+        found = jnp.zeros((rows, LANES), F32)
         for index in range(group):
             own = slice(index * rows, (index + 1) * rows)
-            for order, values in enumerate(columns[g]):
-                stats = jnp.where(lane == order * heads + g * group + index, values[own], stats)
-    out_ref[:, heads * HD :] = stats.astype(BF)
+            first, second, third, fourth = (values[own] for values in columns[g])
+            values = jnp.where(place < 2, jnp.where(place == 0, first, second), jnp.where(place == 2, third, fourth))
+            found = jnp.where(head == g * group + index, values, found)
+        stats.append(found)
+    packed = functools.reduce(jnp.add, stats)
+    for n, out in enumerate(outputs):
+        out[:, heads * HD :] = packed[n * piece : (n + 1) * piece].astype(BF)
 
 
 def attend(chunk, relative, stages, heads, kv_heads, span_len, query, tables, sides):
@@ -194,9 +203,9 @@
     operands = [query, *tables, *[array for side in sides for array in side]]
     return pl.pallas_call(
         functools.partial(attend_kernel, chunk, relative, core, core_stride, heads, kv_heads, span_len),
-        out_shape=jax.ShapeDtypeStruct((rows, heads * HD + LANES), BF),
+        out_shape=(jax.ShapeDtypeStruct((rows // stages[1][1], heads * HD + LANES), BF),) * stages[1][1],
         in_specs=[vmem] * len(operands),
-        out_specs=vmem,
+        out_specs=(vmem,) * stages[1][1],
         cost_estimate=pl.CostEstimate(
             flops=4 * core * rows * heads * HD * slots,
             bytes_accessed=2 * core * sides[0][3].size + 4 * rows * heads * HD,
@@ -289,11 +298,11 @@
     parts = []
     for k in range(outer):
         chunk = swap(rows, k * outer_stride) if k else rows
-        part = attend(k, k * span_count // outer, stages, heads, kv_heads, span_len, chunk, tables, sides)
-        parts.append(swap(part, k * outer_stride) if k else part)
-    kept = merge([parts], inner, heads)
-    received = [swap(kept[i], i * inner_stride) for i in range(1, inner)]
-    (attended,) = merge([[kept[0]] + received], 1, heads, last=True)
+        pieces = attend(k, k * span_count // outer, stages, heads, kv_heads, span_len, chunk, tables, sides)
+        for i, piece in enumerate(pieces):
+            distance = k * outer_stride + i * inner_stride
+            parts.append(swap(piece, distance) if distance else piece)
+    (attended,) = merge([parts], 1, heads, last=True)
     return attended
 
 

time: 31.6 us -> 32.2 us (1.019)
  starting transfers between devices: 14.7 us -> 20.5 us
  waiting for transfers between devices: 9.98 us -> 4.82 us
    ppermute x13 -> x16, starting transfers between devices: 14.7 us -> 20.5 us  [swap(): lax.ppermute(values, 'kv', [(i, i ^ distance) for i in range(devices)])]
    ppermute x13 -> x16, waiting for transfers between devices: 9.98 us -> 4.82 us  [swap(): lax.ppermute(values, 'kv', [(i, i ^ distance) for i in range(devices)])]
    pallas_call x2 -> x1, Pallas kernels: 1.2 us -> 1.01 us  [merge(): pl.pallas_call(functools.partial(merge_kernel, len(groups), count, heads,...]
  transfers between devices with their start and end apart: 13 -> 16, of which waited for: 7 -> 4; matrix products, arithmetic and copies ran while one was open for 0% -> 0% of each run, Pallas kernels for 13% -> 13%
where the time goes in v3:
time: 32.2 us; the launch traced here: 32 us
  starting transfers between devices  20.5 us (64%)
  Pallas kernels  5.07 us (16%)
  waiting for transfers between devices  4.82 us (15%)
  local copies, waits for them, and re-layouts  1.45 us (5%)
    ppermute x16, starting transfers between devices, swap(): lax.ppermute(values, 'kv', [(i, i ^ distance) for i in range(devices)])  20.5 us
    ppermute x16, waiting for transfers between devices, swap(): lax.ppermute(values, 'kv', [(i, i ^ distance) for i in range(devices)])  4.82 us
    pallas_call x4, Pallas kernels, attend(): pl.pallas_call(functools.partial(attend_kernel, chunk, relative, core, co...  3.32 us
    unnamed x15, local copies, waits for them, and re-layouts  1.44 us
    pallas_call x1, Pallas kernels, merge(): pl.pallas_call(functools.partial(merge_kernel, len(groups), count, heads,...  1.01 us
    pallas_call x1, Pallas kernels, prepare(): pl.pallas_call(functools.partial(prepare_kernel, share, span_len, stages)...  0.74 us
  transfers between devices with their start and end apart: 16, of which 4 were waited for; matrix products, arithmetic and copies ran while one was open for 0% of the time, Pallas kernels for 13%

profile of v3, /device:TPU:0, one launch (start us, length us, event | category | flops | bytes accessed | tf_op | source)
XLA Modules:
  0.0 32.0 jit_solution(6519398926293828115)
XLA Ops:
  0.0 0.0 copy-start
  0.0 0.0 copy-start.1
  0.0 3.0 %collective-permute-start = (bf16[8,2048]{1,0:T(8,128)(2,1)}, bf16[8,2048]{1,0:T(8,128)(2,1)S(1)}, u32[]{:S(2)}, u32[]{:S(2)}) collective-permute-start(bf16[8,2048]{1,0:T(8,128)(2,1)} %query_in.1), channel_id=1, source_target_pairs={{0,2},{1,3},{2,0},{3,1},{4,6},{5,7},{6,4},{7,5},{8,10},{9,11},{10,... | collective-permute-start | bytes 98312 | tf_op jit(solution)/shard_map/ppermute | solution.py:40
  3.0 0.0 collective-permute-start.4
  3.0 0.5 %collective-permute-start.5 = (bf16[2,384,512]{2,1,0:T(8,128)(2,1)}, bf16[2,384,512]{2,1,0:T(8,128)(2,1)S(1)}, u32[]{:S(2)}, u32[]{:S(2)}) collective-permute-start(bf16[2,384,512]{2,1,0:T(8,128)(2,1)} %refs_8_.7), channel_id=1, source_target_pairs={{0,1},{1,0},{2,3},{3,2},{4,5},{5,4},{6,7},{7,6},{8,9},{9,8},{10,11... | collective-permute-start | bytes 2359304 | tf_op jit(solution)/shard_map/ppermute | solution.py:40
  3.5 0.0 copy-start.5
  3.5 0.8 %copy-done.5 = bf16[8,2048]{1,0:T(8,128)(2,1)S(1)} copy-done((bf16[8,2048]{1,0:T(8,128)(2,1)S(1)}, bf16[8,2048]{1,0:T(8,128)(2,1)}, u32[]{:S(2)}) %copy-start.5) | copy-done | bytes 32792
  4.3 0.0 copy-start.6
  4.3 0.7 %copy-done.6 = s32[2]{0:T(128)S(1)} copy-done((s32[2]{0:T(128)S(1)}, s32[2]{0:T(128)}, u32[]{:S(2)}) %copy-start.6) | copy-done | bytes 32
  4.9 0.7 %prepare.1 = (bf16[8,2048]{1,0:T(8,128)(2,1)S(1)}, f32[72,128]{1,0:T(8,128)S(1)}, f32[72,128]{1,0:T(8,128)S(1)}, s32[72,128]{1,0:T(8,128)S(1)}) custom-call(s32[2]{0:T(128)S(1)} %copy-done.6, bf16[8,2048]{1,0:T(8,128)(2,1)S(1)} %copy-done.5), custom_call_target="tpu_custom_call" | custom-call | flops 10000000000 | bytes 110592 | tf_op jit(solution)/shard_map/prepare/pallas_call | solution.py:92
  5.7 0.0 copy-start.2
  5.7 0.0 copy-start.3
  5.7 0.0 collective-permute-done
  5.7 0.0 copy-start.4
  5.7 3.7 %collective-permute-start.13 = (bf16[16,2048]{1,0:T(8,128)(2,1)S(1)}, bf16[16,2048]{1,0:T(8,128)(2,1)S(1)}, u32[]{:S(2)}, u32[]{:S(2)}) collective-permute-start(bf16[16,2048]{1,0:T(8,128)(2,1)S(1)} %constant_dynamic-update-slice_fusion.refs_0_), channel_id=1, source_target_pairs={{0,12},{1,13},{2,14},{3,15},{4,8},{5,9},{6,10},{7,11},{8,4},{9,5},... | collective-permute-start | bytes 196616 | tf_op jit(solution)/shard_map/ppermute | solution.py:40
  9.4 0.0 copy-done.2
  9.4 0.0 collective-permute-start.2
  9.4 0.0 copy-done.4
  9.4 0.5 %collective-permute-start.1 = (s32[1,2]{1,0:T(1,128)S(1)}, s32[1,2]{1,0:T(1,128)S(1)}, u32[]{:S(2)}, u32[]{:S(2)}) collective-permute-start(s32[1,2]{1,0:T(1,128)S(1)} %bitcast.1), channel_id=1, source_target_pairs={{0,1},{1,0},{2,3},{3,2},{4,5},{5,4},{6,7},{7,6},{8,9},{9,8},{10,11... | collective-permute-start | bytes 32 | tf_op jit(solution)/shard_map/ppermute | solution.py:40
  9.9 0.8 %collective-permute-done.1.refs_9_ = s32[1,2]{1,0:T(1,128)S(1)} collective-permute-done((s32[1,2]{1,0:T(1,128)S(1)}, s32[1,2]{1,0:T(1,128)S(1)}, u32[]{:S(2)}, u32[]{:S(2)}) %collective-permute-start.1) | collective-permute-done | bytes 40 | tf_op jit(solution)/shard_map/ppermute | solution.py:40
  10.7 0.0 collective-permute-start.10
  10.7 0.0 collective-permute-done.2.refs_10_
  10.7 0.0 copy-done.3
  10.8 0.4 %collective-permute-start.3 = (bf16[8,512]{1,0:T(8,128)(2,1)S(1)}, bf16[8,512]{1,0:T(8,128)(2,1)S(1)}, u32[]{:S(2)}, u32[]{:S(2)}) collective-permute-start(bf16[8,512]{1,0:T(8,128)(2,1)S(1)} %copy-done.3), channel_id=1, source_target_pairs={{0,1},{1,0},{2,3},{3,2},{4,5},{5,4},{6,7},{7,6},{8,9},{9,8},{10,11... | collective-permute-start | bytes 24584 | tf_op jit(solution)/shard_map/ppermute | solution.py:40
  11.2 0.8 %collective-permute-done.3.refs_11_ = bf16[8,512]{1,0:T(8,128)(2,1)S(1)} collective-permute-done((bf16[8,512]{1,0:T(8,128)(2,1)S(1)}, bf16[8,512]{1,0:T(8,128)(2,1)S(1)}, u32[]{:S(2)}, u32[]{:S(2)}) %collective-permute-start.3) | collective-permute-done | bytes 8224 | tf_op jit(solution)/shard_map/ppermute | solution.py:40
  12.0 1.1 %collective-permute-start.7 = (bf16[16,2048]{1,0:T(8,128)(2,1)S(1)}, bf16[16,2048]{1,0:T(8,128)(2,1)S(1)}, u32[]{:S(2)}, u32[]{:S(2)}) collective-permute-start(bf16[16,2048]{1,0:T(8,128)(2,1)S(1)} %constant_dynamic-update-slice_fusion.refs_0_), channel_id=1, source_target_pairs={{0,4},{1,5},{2,6},{3,7},{4,0},{5,1},{6,2},{7,3},{8,12},{9,13},{10,... | collective-permute-start | bytes 196616 | tf_op jit(solution)/shard_map/ppermute | solution.py:40
  13.1 0.0 collective-permute-done.13.refs_0_
  13.1 0.0 collective-permute-done.4.refs_12_
  13.1 0.0 collective-permute-done.5.refs_13_
  13.1 0.0 copy-done
  13.1 0.0 copy-done.1
  13.1 0.8 %attend.7 = (bf16[8,2176]{1,0:T(8,128)(2,1)S(1)}, bf16[8,2176]{1,0:T(8,128)(2,1)S(1)}) custom-call(bf16[16,2048]{1,0:T(8,128)(2,1)S(1)} %collective-permute-done.13.refs_0_, f32[72,128]{1,0:T(8,128)S(1)} %get-tuple-element.18.refs_1_, f32[72,128]{1,0:T(8,128)S(1)} %get-tuple-element.19.refs_2_, s32[72,128]{1,0:T(8,128)S(1)} %get-tuple-element.20.refs_3_, ...), custom_call_target="tpu_custom_call" | custom-call | flops 100663296 | bytes 1703936 | tf_op jit(solution)/shard_map/attend/pallas_call | solution.py:204
  13.9 3.3 %collective-permute-start.14 = (bf16[8,2176]{1,0:T(8,128)(2,1)S(1)}, bf16[8,2176]{1,0:T(8,128)(2,1)S(1)}, u32[]{:S(2)}, u32[]{:S(2)}) collective-permute-start(bf16[8,2176]{1,0:T(8,128)(2,1)S(1)} %get-tuple-element.27), channel_id=1, source_target_pairs={{0,12},{1,13},{2,14},{3,15},{4,8},{5,9},{6,10},{7,11},{8,4},{9,5},... | collective-permute-start | bytes 104456 | tf_op jit(solution)/shard_map/ppermute | solution.py:40
  17.2 1.2 %collective-permute-start.15 = (bf16[8,2176]{1,0:T(8,128)(2,1)S(1)}, bf16[8,2176]{1,0:T(8,128)(2,1)S(1)}, u32[]{:S(2)}, u32[]{:S(2)}) collective-permute-start(bf16[8,2176]{1,0:T(8,128)(2,1)S(1)} %get-tuple-element.28), channel_id=1, source_target_pairs={{0,14},{1,15},{2,12},{3,13},{4,10},{5,11},{6,8},{7,9},{8,6},{9,7},... | collective-permute-start | bytes 104456 | tf_op jit(solution)/shard_map/ppermute | solution.py:40
  18.5 0.0 collective-permute-done.10.refs_0_
  18.5 0.8 %attend.6 = (bf16[8,2176]{1,0:T(8,128)(2,1)S(1)}, bf16[8,2176]{1,0:T(8,128)(2,1)S(1)}) custom-call(bf16[16,2048]{1,0:T(8,128)(2,1)S(1)} %collective-permute-done.10.refs_0_, f32[72,128]{1,0:T(8,128)S(1)} %get-tuple-element.18.refs_1_, f32[72,128]{1,0:T(8,128)S(1)} %get-tuple-element.19.refs_2_, s32[72,128]{1,0:T(8,128)S(1)} %get-tuple-element.20.refs_3_, ...), custom_call_target="tpu_custom_call" | custom-call | flops 100663296 | bytes 1703936 | tf_op jit(solution)/shard_map/attend/pallas_call | solution.py:204
  19.3 0.2 collective-permute-start.11
  19.5 3.1 %collective-permute-start.12 = (bf16[8,2176]{1,0:T(8,128)(2,1)S(1)}, bf16[8,2176]{1,0:T(8,128)(2,1)S(1)}, u32[]{:S(2)}, u32[]{:S(2)}) collective-permute-start(bf16[8,2176]{1,0:T(8,128)(2,1)S(1)} %get-tuple-element.26), channel_id=1, source_target_pairs={{0,10},{1,11},{2,8},{3,9},{4,14},{5,15},{6,12},{7,13},{8,2},{9,3},... | collective-permute-start | bytes 104456 | tf_op jit(solution)/shard_map/ppermute | solution.py:40
  22.5 0.0 collective-permute-done.7.refs_0_
  22.5 0.8 %attend.5 = (bf16[8,2176]{1,0:T(8,128)(2,1)S(1)}, bf16[8,2176]{1,0:T(8,128)(2,1)S(1)}) custom-call(bf16[16,2048]{1,0:T(8,128)(2,1)S(1)} %collective-permute-done.7.refs_0_, f32[72,128]{1,0:T(8,128)S(1)} %get-tuple-element.18.refs_1_, f32[72,128]{1,0:T(8,128)S(1)} %get-tuple-element.19.refs_2_, s32[72,128]{1,0:T(8,128)S(1)} %get-tuple-element.20.refs_3_, ...), custom_call_target="tpu_custom_call" | custom-call | flops 100663296 | bytes 1703936 | tf_op jit(solution)/shard_map/attend/pallas_call | solution.py:204
  23.4 1.0 %collective-permute-start.8 = (bf16[8,2176]{1,0:T(8,128)(2,1)S(1)}, bf16[8,2176]{1,0:T(8,128)(2,1)S(1)}, u32[]{:S(2)}, u32[]{:S(2)}) collective-permute-start(bf16[8,2176]{1,0:T(8,128)(2,1)S(1)} %get-tuple-element.23), channel_id=1, source_target_pairs={{0,4},{1,5},{2,6},{3,7},{4,0},{5,1},{6,2},{7,3},{8,12},{9,13},{10,... | collective-permute-start | bytes 104456 | tf_op jit(solution)/shard_map/ppermute | solution.py:40
  24.4 0.8 %attend.4 = (bf16[8,2176]{1,0:T(8,128)(2,1)S(1)}, bf16[8,2176]{1,0:T(8,128)(2,1)S(1)}) custom-call(bf16[16,2048]{1,0:T(8,128)(2,1)S(1)} %constant_dynamic-update-slice_fusion.refs_0_, f32[72,128]{1,0:T(8,128)S(1)} %get-tuple-element.18.refs_1_, f32[72,128]{1,0:T(8,128)S(1)} %get-tuple-element.19.refs_2_, s32[72,128]{1,0:T(8,128)S(1)} %get-tuple-element.20.refs_3_, ...), custom_call_target="tpu_custom_call" | custom-call | flops 100663296 | bytes 1703936 | tf_op jit(solution)/shard_map/attend/pallas_call | solution.py:204
  25.2 0.0 collective-permute-done.14.refs_6_
  25.2 1.8 %collective-permute-start.9 = (bf16[8,2176]{1,0:T(8,128)(2,1)S(1)}, bf16[8,2176]{1,0:T(8,128)(2,1)S(1)}, u32[]{:S(2)}, u32[]{:S(2)}) collective-permute-start(bf16[8,2176]{1,0:T(8,128)(2,1)S(1)} %get-tuple-element.24), channel_id=1, source_target_pairs={{0,6},{1,7},{2,4},{3,5},{4,2},{5,3},{6,0},{7,1},{8,14},{9,15},{10,... | collective-permute-start | bytes 104456 | tf_op jit(solution)/shard_map/ppermute | solution.py:40
  27.0 0.0 collective-permute-done.15.refs_7_
  27.0 0.8 %collective-permute-start.6 = (bf16[8,2176]{1,0:T(8,128)(2,1)S(1)}, bf16[8,2176]{1,0:T(8,128)(2,1)S(1)}, u32[]{:S(2)}, u32[]{:S(2)}) collective-permute-start(bf16[8,2176]{1,0:T(8,128)(2,1)S(1)} %get-tuple-element.22), channel_id=1, source_target_pairs={{0,2},{1,3},{2,0},{3,1},{4,6},{5,7},{6,4},{7,5},{8,10},{9,11},{10,... | collective-permute-start | bytes 104456 | tf_op jit(solution)/shard_map/ppermute | solution.py:40
  27.8 0.0 collective-permute-done.11.refs_4_
  27.8 0.0 collective-permute-done.12.refs_5_
  27.8 0.0 collective-permute-done.8.refs_2_
  27.8 2.3 %collective-permute-done.9.refs_3_ = bf16[8,2176]{1,0:T(8,128)(2,1)S(1)} collective-permute-done((bf16[8,2176]{1,0:T(8,128)(2,1)S(1)}, bf16[8,2176]{1,0:T(8,128)(2,1)S(1)}, u32[]{:S(2)}, u32[]{:S(2)}) %collective-permute-start.9) | collective-permute-done | bytes 34848 | tf_op jit(solution)/shard_map/ppermute | solution.py:40
  30.1 0.8 %collective-permute-done.6.refs_1_ = bf16[8,2176]{1,0:T(8,128)(2,1)S(1)} collective-permute-done((bf16[8,2176]{1,0:T(8,128)(2,1)S(1)}, bf16[8,2176]{1,0:T(8,128)(2,1)S(1)}, u32[]{:S(2)}, u32[]{:S(2)}) %collective-permute-start.6) | collective-permute-done | bytes 34848 | tf_op jit(solution)/shard_map/ppermute | solution.py:40
  31.0 1.0 %merge.1 = bf16[8,2048]{1,0:T(8,128)(2,1)} custom-call(bf16[8,2176]{1,0:T(8,128)(2,1)S(1)} %get-tuple-element.21.refs_0_, bf16[8,2176]{1,0:T(8,128)(2,1)S(1)} %collective-permute-done.6.refs_1_, bf16[8,2176]{1,0:T(8,128)(2,1)S(1)} %collective-permute-done.8.refs_2_, bf16[8,2176]{1,0:T(8,128)(2,1)S(1)} %collective-permute-done.9.refs_3_, ...), custom_call_target="tpu_custom_call" | custom-call | flops 524288 | bytes 294912 | tf_op jit(solution)/shard_map/merge/pallas_call | solution.py:265
  (2 shorter events, 0.0 us)
Async XLA Ops:
  0.0 13.1 %copy-start = (bf16[2,384,512]{2,1,0:T(8,128)(2,1)S(1)}, bf16[2,384,512]{2,1,0:T(8,128)(2,1)}, u32[]{:S(2)}) copy-start(bf16[2,384,512]{2,1,0:T(8,128)(2,1)} %refs_7_.7) | copy-start | bytes 2359300
  0.0 13.1 %copy-start.1 = (bf16[2,384,512]{2,1,0:T(8,128)(2,1)S(1)}, bf16[2,384,512]{2,1,0:T(8,128)(2,1)}, u32[]{:S(2)}) copy-start(bf16[2,384,512]{2,1,0:T(8,128)(2,1)} %refs_8_.7) | copy-start | bytes 2359300
  0.0 5.7 %collective-permute-start = (bf16[8,2048]{1,0:T(8,128)(2,1)}, bf16[8,2048]{1,0:T(8,128)(2,1)S(1)}, u32[]{:S(2)}, u32[]{:S(2)}) collective-permute-start(bf16[8,2048]{1,0:T(8,128)(2,1)} %query_in.1), channel_id=1, source_target_pairs={{0,2},{1,3},{2,0},{3,1},{4,6},{5,7},{6,4},{7,5},{8,10},{9,11},{10,... | collective-permute-start | bytes 98312 | tf_op jit(solution)/shard_map/ppermute | solution.py:40
  3.0 10.1 %collective-permute-start.4 = (bf16[2,384,512]{2,1,0:T(8,128)(2,1)}, bf16[2,384,512]{2,1,0:T(8,128)(2,1)S(1)}, u32[]{:S(2)}, u32[]{:S(2)}) collective-permute-start(bf16[2,384,512]{2,1,0:T(8,128)(2,1)} %refs_7_.7), channel_id=1, source_target_pairs={{0,1},{1,0},{2,3},{3,2},{4,5},{5,4},{6,7},{7,6},{8,9},{9,8},{10,11... | collective-permute-start | bytes 2359304 | tf_op jit(solution)/shard_map/ppermute | solution.py:40
  3.0 10.1 %collective-permute-start.5 = (bf16[2,384,512]{2,1,0:T(8,128)(2,1)}, bf16[2,384,512]{2,1,0:T(8,128)(2,1)S(1)}, u32[]{:S(2)}, u32[]{:S(2)}) collective-permute-start(bf16[2,384,512]{2,1,0:T(8,128)(2,1)} %refs_8_.7), channel_id=1, source_target_pairs={{0,1},{1,0},{2,3},{3,2},{4,5},{5,4},{6,7},{7,6},{8,9},{9,8},{10,11... | collective-permute-start | bytes 2359304 | tf_op jit(solution)/shard_map/ppermute | solution.py:40
  3.5 0.8 %copy-start.5 = (bf16[8,2048]{1,0:T(8,128)(2,1)S(1)}, bf16[8,2048]{1,0:T(8,128)(2,1)}, u32[]{:S(2)}) copy-start(bf16[8,2048]{1,0:T(8,128)(2,1)} %query_in.1) | copy-start | bytes 98308
  4.3 0.7 %copy-start.6 = (s32[2]{0:T(128)S(1)}, s32[2]{0:T(128)}, u32[]{:S(2)}) copy-start(s32[2]{0:T(128)} %start_ref.1) | copy-start | bytes 28
  5.7 3.7 %copy-start.2 = (bf16[8,512]{1,0:T(8,128)(2,1)S(1)}, bf16[8,512]{1,0:T(8,128)(2,1)}, u32[]{:S(2)}) copy-start(bf16[8,512]{1,0:T(8,128)(2,1)} %refs_5_.7) | copy-start | bytes 24580
  5.7 5.1 %copy-start.3 = (bf16[8,512]{1,0:T(8,128)(2,1)S(1)}, bf16[8,512]{1,0:T(8,128)(2,1)}, u32[]{:S(2)}) copy-start(bf16[8,512]{1,0:T(8,128)(2,1)} %refs_6_.7) | copy-start | bytes 24580
  5.7 3.7 %copy-start.4 = (s32[2,1]{0,1:T(1,128)S(1)}, s32[2,1]{0,1:T(1,128)}, u32[]{:S(2)}) copy-start(s32[2,1]{0,1:T(1,128)} %param.12) | copy-start | bytes 28
  5.7 7.3 %collective-permute-start.13 = (bf16[16,2048]{1,0:T(8,128)(2,1)S(1)}, bf16[16,2048]{1,0:T(8,128)(2,1)S(1)}, u32[]{:S(2)}, u32[]{:S(2)}) collective-permute-start(bf16[16,2048]{1,0:T(8,128)(2,1)S(1)} %constant_dynamic-update-slice_fusion.refs_0_), channel_id=1, source_target_pairs={{0,12},{1,13},{2,14},{3,15},{4,8},{5,9},{6,10},{7,11},{8,4},{9,5},... | collective-permute-start | bytes 196616 | tf_op jit(solution)/shard_map/ppermute | solution.py:40
  9.4 1.3 %collective-permute-start.2 = (bf16[8,512]{1,0:T(8,128)(2,1)S(1)}, bf16[8,512]{1,0:T(8,128)(2,1)S(1)}, u32[]{:S(2)}, u32[]{:S(2)}) collective-permute-start(bf16[8,512]{1,0:T(8,128)(2,1)S(1)} %copy-done.2), channel_id=1, source_target_pairs={{0,1},{1,0},{2,3},{3,2},{4,5},{5,4},{6,7},{7,6},{8,9},{9,8},{10,11... | collective-permute-start | bytes 24584 | tf_op jit(solution)/shard_map/ppermute | solution.py:40
  9.4 1.3 %collective-permute-start.1 = (s32[1,2]{1,0:T(1,128)S(1)}, s32[1,2]{1,0:T(1,128)S(1)}, u32[]{:S(2)}, u32[]{:S(2)}) collective-permute-start(s32[1,2]{1,0:T(1,128)S(1)} %bitcast.1), channel_id=1, source_target_pairs={{0,1},{1,0},{2,3},{3,2},{4,5},{5,4},{6,7},{7,6},{8,9},{9,8},{10,11... | collective-permute-start | bytes 32 | tf_op jit(solution)/shard_map/ppermute | solution.py:40
  10.7 7.7 %collective-permute-start.10 = (bf16[16,2048]{1,0:T(8,128)(2,1)S(1)}, bf16[16,2048]{1,0:T(8,128)(2,1)S(1)}, u32[]{:S(2)}, u32[]{:S(2)}) collective-permute-start(bf16[16,2048]{1,0:T(8,128)(2,1)S(1)} %constant_dynamic-update-slice_fusion.refs_0_), channel_id=1, source_target_pairs={{0,8},{1,9},{2,10},{3,11},{4,12},{5,13},{6,14},{7,15},{8,0},{9,1},... | collective-permute-start | bytes 196616 | tf_op jit(solution)/shard_map/ppermute | solution.py:40
  10.8 1.2 %collective-permute-start.3 = (bf16[8,512]{1,0:T(8,128)(2,1)S(1)}, bf16[8,512]{1,0:T(8,128)(2,1)S(1)}, u32[]{:S(2)}, u32[]{:S(2)}) collective-permute-start(bf16[8,512]{1,0:T(8,128)(2,1)S(1)} %copy-done.3), channel_id=1, source_target_pairs={{0,1},{1,0},{2,3},{3,2},{4,5},{5,4},{6,7},{7,6},{8,9},{9,8},{10,11... | collective-permute-start | bytes 24584 | tf_op jit(solution)/shard_map/ppermute | solution.py:40
  12.0 10.5 %collective-permute-start.7 = (bf16[16,2048]{1,0:T(8,128)(2,1)S(1)}, bf16[16,2048]{1,0:T(8,128)(2,1)S(1)}, u32[]{:S(2)}, u32[]{:S(2)}) collective-permute-start(bf16[16,2048]{1,0:T(8,128)(2,1)S(1)} %constant_dynamic-update-slice_fusion.refs_0_), channel_id=1, source_target_pairs={{0,4},{1,5},{2,6},{3,7},{4,0},{5,1},{6,2},{7,3},{8,12},{9,13},{10,... | collective-permute-start | bytes 196616 | tf_op jit(solution)/shard_map/ppermute | solution.py:40
  13.9 11.3 %collective-permute-start.14 = (bf16[8,2176]{1,0:T(8,128)(2,1)S(1)}, bf16[8,2176]{1,0:T(8,128)(2,1)S(1)}, u32[]{:S(2)}, u32[]{:S(2)}) collective-permute-start(bf16[8,2176]{1,0:T(8,128)(2,1)S(1)} %get-tuple-element.27), channel_id=1, source_target_pairs={{0,12},{1,13},{2,14},{3,15},{4,8},{5,9},{6,10},{7,11},{8,4},{9,5},... | collective-permute-start | bytes 104456 | tf_op jit(solution)/shard_map/ppermute | solution.py:40
  17.2 9.8 %collective-permute-start.15 = (bf16[8,2176]{1,0:T(8,128)(2,1)S(1)}, bf16[8,2176]{1,0:T(8,128)(2,1)S(1)}, u32[]{:S(2)}, u32[]{:S(2)}) collective-permute-start(bf16[8,2176]{1,0:T(8,128)(2,1)S(1)} %get-tuple-element.28), channel_id=1, source_target_pairs={{0,14},{1,15},{2,12},{3,13},{4,10},{5,11},{6,8},{7,9},{8,6},{9,7},... | collective-permute-start | bytes 104456 | tf_op jit(solution)/shard_map/ppermute | solution.py:40
  19.3 8.5 %collective-permute-start.11 = (bf16[8,2176]{1,0:T(8,128)(2,1)S(1)}, bf16[8,2176]{1,0:T(8,128)(2,1)S(1)}, u32[]{:S(2)}, u32[]{:S(2)}) collective-permute-start(bf16[8,2176]{1,0:T(8,128)(2,1)S(1)} %get-tuple-element.25), channel_id=1, source_target_pairs={{0,8},{1,9},{2,10},{3,11},{4,12},{5,13},{6,14},{7,15},{8,0},{9,1},... | collective-permute-start | bytes 104456 | tf_op jit(solution)/shard_map/ppermute | solution.py:40
  19.5 8.4 %collective-permute-start.12 = (bf16[8,2176]{1,0:T(8,128)(2,1)S(1)}, bf16[8,2176]{1,0:T(8,128)(2,1)S(1)}, u32[]{:S(2)}, u32[]{:S(2)}) collective-permute-start(bf16[8,2176]{1,0:T(8,128)(2,1)S(1)} %get-tuple-element.26), channel_id=1, source_target_pairs={{0,10},{1,11},{2,8},{3,9},{4,14},{5,15},{6,12},{7,13},{8,2},{9,3},... | collective-permute-start | bytes 104456 | tf_op jit(solution)/shard_map/ppermute | solution.py:40
  23.4 4.5 %collective-permute-start.8 = (bf16[8,2176]{1,0:T(8,128)(2,1)S(1)}, bf16[8,2176]{1,0:T(8,128)(2,1)S(1)}, u32[]{:S(2)}, u32[]{:S(2)}) collective-permute-start(bf16[8,2176]{1,0:T(8,128)(2,1)S(1)} %get-tuple-element.23), channel_id=1, source_target_pairs={{0,4},{1,5},{2,6},{3,7},{4,0},{5,1},{6,2},{7,3},{8,12},{9,13},{10,... | collective-permute-start | bytes 104456 | tf_op jit(solution)/shard_map/ppermute | solution.py:40
  25.2 4.9 %collective-permute-start.9 = (bf16[8,2176]{1,0:T(8,128)(2,1)S(1)}, bf16[8,2176]{1,0:T(8,128)(2,1)S(1)}, u32[]{:S(2)}, u32[]{:S(2)}) collective-permute-start(bf16[8,2176]{1,0:T(8,128)(2,1)S(1)} %get-tuple-element.24), channel_id=1, source_target_pairs={{0,6},{1,7},{2,4},{3,5},{4,2},{5,3},{6,0},{7,1},{8,14},{9,15},{10,... | collective-permute-start | bytes 104456 | tf_op jit(solution)/shard_map/ppermute | solution.py:40
  27.0 3.9 %collective-permute-start.6 = (bf16[8,2176]{1,0:T(8,128)(2,1)S(1)}, bf16[8,2176]{1,0:T(8,128)(2,1)S(1)}, u32[]{:S(2)}, u32[]{:S(2)}) collective-permute-start(bf16[8,2176]{1,0:T(8,128)(2,1)S(1)} %get-tuple-element.22), channel_id=1, source_target_pairs={{0,2},{1,3},{2,0},{3,1},{4,6},{5,7},{6,4},{7,5},{8,10},{9,11},{10,... | collective-permute-start | bytes 104456 | tf_op jit(solution)/shard_map/ppermute | solution.py:40
